TPU v7x, 32 devices: a whole 2x2x4 slice. The times are simulated.
32 devices in a mesh: dp: 2 (over x), ep: 16 (over z, y, core).
Axes of the slice: x: 2, y: 2, z: 4, core: 2. Of those that a mesh axis runs over, the one named last changes fastest.
Arguments:
- tokens: bfloat16 [8192, 512], P(('dp', 'ep')), parts along dimension 0, may hold values from -6 to 6
- routes: int32 [8192, 2], P(('dp', 'ep')), parts along dimension 0, may hold values from 0 to 15, all different within a row; in each aligned block of 256 rows (0 to 255, 256 to 511, ...) at most 64 rows name the same one
- capacity: int32 [16], replicated, may hold values from 32 to 64, as said below
- expert_in: bfloat16 [16, 512, 2048], P('ep'), may hold values from -0.25 to 0.25
- expert_out: bfloat16 [16, 2048, 512], P('ep'), may hold values from -0.125 to 0.125
- shared_in: bfloat16 [2, 2048, 512], P(None, 'ep'), may hold values from -0.25 to 0.25
- shared_out: bfloat16 [2, 2048, 512], P(None, 'ep'), may hold values from -0.125 to 0.125
- route_gate: bfloat16 [16, 6144], P('ep'), may hold values from -0.25 to 0.25
- shared_gate: bfloat16 [2, 6144], replicated, may hold values from -0.25 to 0.25
Outputs:
- mixed: bfloat16 [8192, 12, 512], P(('dp', 'ep')), parts along dimension 0
There are 2 independent parts, one for each index of `dp`. A program takes and returns all parts, laid end to end along the dimension named above; an argument that names none is the same for every part. Nothing has to cross between parts.
Inputs may be any that keep to these rules, and one draw needn't show every extreme that they name: `routes`: each sample names 2 different experts. Within each device's block of 256 samples no expert is named more than 64 times. `capacity`: some expert accepts exactly 64 rows.
All inputs are finite; a program needn't handle non-finite values.
Results may differ from a plain program's by a relative error of at most 0.0054.
Values may be sent and summed in bfloat16 or wider, within the bound.
No kernel may reach another device: no remote copies, remote signals or barrier semaphores. Data moves between devices by JAX's collectives and lax.ppermute only.
A program may use at most 64 MiB of HBM per device.

v0:
```python
import functools

import jax
import jax.numpy as jnp
from jax import lax
from jax.experimental import pallas as pl
from jax.experimental.pallas import tpu as pltpu
from jax.sharding import PartitionSpec as P


BF, F32, I32 = jnp.bfloat16, jnp.float32, jnp.int32
GRANT = 24 << 20
PAD = 16


def whole(shape):
    return pl.BlockSpec(shape, lambda *_: (0,) * len(shape))


def call(kernel, out_shape, **kw):
    return pl.pallas_call(
        kernel,
        out_shape=out_shape,
        compiler_params=pltpu.CompilerParams(vmem_limit_bytes=GRANT),
        **kw,
    )


def in_hbm(x):
    return pltpu.with_memory_space_constraint(x, pltpu.HBM)


def cost(flops, size):
    return pl.CostEstimate(flops=int(flops), bytes_accessed=int(size), transcendentals=0)


def dot_t(a, b):
    return lax.dot_general(a, b, (((1,), (1,)), ((), ())), preferred_element_type=F32)


def pack_kernel(tasks, me_ref, pick_ref, *refs):
    (in_ref, out_ref, gate_ref, t_ref, r_ref, c_ref, packed_ref, sent_ref, limit_ref) = refs[:9]
    gates, routes, caps, sems = refs[9:]
    units, width = in_ref.shape[1:]
    count = t_ref.shape[0]
    pick, me = pick_ref[0], me_ref[0]
    copies = [
        pltpu.make_async_copy(source, target, sems.at[i])
        for i, (source, target) in enumerate(
            (
                (r_ref, routes),
                (c_ref, caps),
                (gate_ref, gates),
                (t_ref, sent_ref.at[0:count]),
                (in_ref.at[pick], packed_ref.at[0:units]),
                (out_ref.at[pick], packed_ref.at[units : 2 * units]),
            )
        )
    ]
    for copy in copies:
        copy.start()
    for copy in copies[:3]:
        copy.wait()
    blank = jnp.zeros((PAD - routes.shape[0], count), F32)
    named = jnp.concatenate([routes[...].astype(F32), blank], axis=0).astype(BF)
    sent_ref[count:] = jnp.concatenate([named, jnp.zeros((PAD, width - count), BF)], axis=1)
    rows = [gates[:, s * width : (s + 1) * width] for s in range(tasks)]
    rows.append(jnp.zeros((packed_ref.shape[0] - 2 * units - tasks, width), BF))
    packed_ref[2 * units :] = jnp.concatenate(rows, axis=0)
    ids = lax.broadcasted_iota(I32, limit_ref.shape, 0)
    limit = jnp.zeros(limit_ref.shape, F32)
    for q in range(limit_ref.shape[0]):
        limit = jnp.where(ids == q, caps[q ^ me].astype(F32), limit)
    limit_ref[...] = limit
    for copy in copies[3:]:
        copy.wait()


def pack(me, pick, shared_in, shared_out, route_gate, tokens, routes, capacity, tasks):
    _, units, width = shared_in.shape
    count = tokens.shape[0]
    rows = 2 * units + -(-tasks // PAD) * PAD
    smem = pl.BlockSpec(memory_space=pltpu.SMEM)
    vmem = pl.BlockSpec(memory_space=pltpu.VMEM)
    return call(
        functools.partial(pack_kernel, tasks),
        [
            jax.ShapeDtypeStruct((rows, width), BF),
            jax.ShapeDtypeStruct((count + PAD, width), BF),
            jax.ShapeDtypeStruct((capacity.shape[0], count), F32),
        ],
        in_specs=[smem, smem] + [pl.BlockSpec(memory_space=pltpu.HBM)] * 6,
        out_specs=[vmem] * 3,
        scratch_shapes=[
            pltpu.VMEM(route_gate.shape, BF),
            pltpu.VMEM(routes.shape, I32),
            pltpu.SMEM(capacity.shape, I32),
            pltpu.SemaphoreType.DMA((6,)),
        ],
    )(me, pick, *map(in_hbm, (shared_in, shared_out, route_gate, tokens, routes, capacity)))


def dispatch_kernel(targets, depth, me_ref, limit_ref, t0_ref, t1_ref, *outs):
    me = me_ref[0]
    experts, count = limit_ref.shape
    ids = lax.broadcasted_iota(I32, (experts, count), 0)
    earlier = lax.broadcasted_iota(I32, (count, count), 0) < lax.broadcasted_iota(
        I32, (count, count), 1
    )
    upper = jnp.where(earlier, 1.0, 0.0).astype(BF)
    slot = lax.broadcasted_iota(I32, (depth, count), 0).astype(F32)
    codes, keeps = [], []
    for side, sent in enumerate((t0_ref, t1_ref)):
        rel = routes_of(sent, count) ^ me
        named = [rel[k : k + 1] == ids for k in range(2)]
        chosen = jnp.logical_or(*named)
        before = jnp.dot(jnp.where(chosen, 1.0, 0.0).astype(BF), upper, preferred_element_type=F32)
        kept = jnp.logical_and(chosen, before < limit_ref[...])
        ranked = jnp.where(kept, before, -1.0)
        table = jnp.concatenate(
            [
                jnp.where(ranked[2 * m : 2 * m + 1] == slot, 1.0, 0.0).astype(BF)
                for m in range(targets)
            ],
            axis=0,
        )
        picked = jnp.dot(table, sent[0:count], preferred_element_type=F32).astype(BF)
        for m in range(targets):
            outs[m][side * depth : (side + 1) * depth] = picked[m * depth : (m + 1) * depth]
        for k, here in enumerate(named):
            rank = jnp.sum(jnp.where(here, ranked, 0.0), axis=0, keepdims=True)
            keep = rank >= 0.0
            mine = jnp.logical_and(keep, (rel[k : k + 1] & 1) == 0)
            place = ((rel[k : k + 1] >> 1) * depth).astype(F32) + rank
            codes.append(jnp.where(mine, place, -1.0))
            if side == 0:
                keeps.append(jnp.where(keep, 1.0, 0.0))
    if len(outs) > targets:
        blank = jnp.zeros((8 - len(codes) - len(keeps), count), F32)
        outs[targets][...] = jnp.concatenate(codes + keeps + [blank], axis=0)


def routes_of(sent, count):
    return sent[count:, 0:count].astype(F32)[0:2].astype(I32)


def dispatch(me, limit, t0, t1, depth, slots):
    targets = limit.shape[0] // 4
    count, width = limit.shape[1], t0.shape[1]
    smem = pl.BlockSpec(memory_space=pltpu.SMEM)
    vmem = pl.BlockSpec(memory_space=pltpu.VMEM)
    return call(
        functools.partial(dispatch_kernel, targets, depth),
        [jax.ShapeDtypeStruct((2 * depth, width), BF)] * targets
        + [jax.ShapeDtypeStruct((8, count), F32)] * slots,
        in_specs=[smem] + [vmem] * 3,
        out_specs=[vmem] * (targets + slots),
        cost_estimate=cost(4 * targets * depth * count * width, 6 * count * width),
    )(me, limit, t0, t1)


def load_kernel(a_ref, b_ref, a_out, b_out, sems):
    parts = sems.shape[1]
    copies = []
    for j, (source, target) in enumerate(((a_ref, a_out), (b_ref, b_out))):
        rows = source.shape[0] // parts
        for i in range(parts):
            piece = pl.ds(i * rows, rows)
            copies.append(
                pltpu.make_async_copy(source.at[piece], target.at[piece], sems.at[j, i])
            )
    for copy in copies:
        copy.start()
    for copy in copies:
        copy.wait()


def load(a, b):
    return call(
        load_kernel,
        [jax.ShapeDtypeStruct(a.shape, a.dtype), jax.ShapeDtypeStruct(b.shape, b.dtype)],
        in_specs=[pl.BlockSpec(memory_space=pltpu.HBM)] * 2,
        out_specs=[pl.BlockSpec(memory_space=pltpu.VMEM)] * 2,
        scratch_shapes=[pltpu.SemaphoreType.DMA((2, 4))],
        cost_estimate=cost(0, 4 * (a.size + b.size)),
    )(in_hbm(a), in_hbm(b))


def expert_kernel(blocks, w1_ref, w2_ref, *refs):
    ins, outs, x_ref, acc_ref = refs[:blocks], refs[blocks : 2 * blocks], refs[-2], refs[-1]
    step = pl.program_id(0)
    rows = ins[0].shape[0]

    @pl.when(step == 0)
    def _():
        for i in range(blocks):
            x_ref[i * rows : (i + 1) * rows] = ins[i][...]

    hidden = jax.nn.gelu(jnp.dot(x_ref[...], w1_ref[...], preferred_element_type=F32)).astype(BF)
    part = jnp.dot(hidden, w2_ref[...], preferred_element_type=F32)

    @pl.when(step == 0)
    def _():
        acc_ref[...] = part

    @pl.when(step > 0)
    def _():
        acc_ref[...] += part

    @pl.when(step == pl.num_programs(0) - 1)
    def _():
        for i in range(blocks):
            outs[i][...] = acc_ref[i * rows : (i + 1) * rows].astype(BF)


def expert(w1, w2, xs, tile=1024):
    width, units = w1.shape
    tile = min(tile, units)
    rows = xs[0].shape[0]
    total = rows * len(xs)
    row_spec = whole((rows, width))
    return call(
        functools.partial(expert_kernel, len(xs)),
        [jax.ShapeDtypeStruct((rows, width), BF)] * len(xs),
        grid=(units // tile,),
        in_specs=[
            pl.BlockSpec((width, tile), lambda i: (0, i)),
            pl.BlockSpec((tile, width), lambda i: (i, 0)),
        ]
        + [row_spec] * len(xs),
        out_specs=[row_spec] * len(xs),
        scratch_shapes=[pltpu.VMEM((total, width), BF), pltpu.VMEM((total, width), F32)],
        cost_estimate=cost(4 * total * width * units, 4 * width * (units + total)),
    )(w1, w2, *xs)


def shared_kernel(shards, units, last, group, *refs):
    ins, tokens, refs = refs[:shards], refs[shards : shards + 4], refs[shards + 4 :]
    rows = refs[-1].shape[0] // 4
    count = rows
    x_ref = refs[-1]
    for i, t in enumerate(tokens):
        x_ref[i * rows : (i + 1) * rows] = t[0:count]
    total = None
    for first in range(0, shards, group):
        part = ins[first : first + group]
        up = jnp.concatenate([w[0:units] for w in part], axis=0)
        down = jnp.concatenate([w[units : 2 * units] for w in part], axis=0)
        hidden = jax.nn.gelu(dot_t(x_ref[...], up)).astype(BF)
        term = jnp.dot(hidden, down, preferred_element_type=F32)
        total = term if total is None else total + term
    gates = jnp.concatenate([w[2 * units :] for w in ins], axis=0)
    if last:
        before, early, keep_ref, send_ref = refs[:4]
        total = total + before[...]
        keep_ref[...] = total[0 : 2 * rows].astype(BF)
        send_ref[0 : 2 * rows] = total[2 * rows :].astype(BF)
        send_ref[2 * rows : 2 * rows + gates.shape[0]] = early[...]
        send_ref[2 * rows + gates.shape[0] :] = gates
    else:
        refs[0][...] = total
        refs[1][...] = gates


def shared(shards, units, tokens, count, carried=()):
    width = shards[0].shape[1]
    gates = len(shards) * (shards[0].shape[0] - 2 * units)
    vmem = pl.BlockSpec(memory_space=pltpu.VMEM)
    if carried:
        shapes = [((2 * count, width), BF), ((2 * count + 2 * gates, width), BF)]
    else:
        shapes = [((4 * count, width), F32), ((gates, width), BF)]
    group = max(1, min(len(shards), 256 // units))
    return call(
        functools.partial(shared_kernel, len(shards), units, bool(carried), group),
        [jax.ShapeDtypeStruct(*shape) for shape in shapes],
        in_specs=[vmem] * (len(shards) + 4 + len(carried)),
        out_specs=[vmem] * 2,
        scratch_shapes=[pltpu.VMEM((4 * count, width), BF)],
        cost_estimate=cost(
            16 * count * width * units * len(shards), 4 * len(shards) * units * width
        ),
    )(*shards, *tokens, *carried)


def weight_kernel(tasks, order, me_ref, pick_ref, rows_ref, t_ref, g0_ref, g1_ref, s_ref, w_ref):
    count = rows_ref.shape[1]
    width = t_ref.shape[1]
    me, pick = me_ref[0], pick_ref[0]
    rel = routes_of(t_ref, count) ^ me
    tokens = t_ref[0:count]
    gates = -(-tasks // PAD) * PAD
    total = len(order) * gates

    def logits(g):
        return dot_t(g, tokens).astype(BF).astype(F32)

    chosen = [jnp.zeros((gates, count), F32) for _ in range(2)]
    for parity, ref in ((0, g0_ref), (1, g1_ref)):
        found = logits(ref[ref.shape[0] - total :])
        for p, q in enumerate(order):
            for k in range(2):
                chosen[k] = jnp.where(
                    rel[k : k + 1] == q ^ parity, found[p * gates : (p + 1) * gates], chosen[k]
                )
    values = [rows_ref[4 + k : 5 + k] * jax.nn.sigmoid(chosen[k]) for k in range(2)]
    own = []
    for j in range(2):
        gate = jnp.concatenate(
            [s_ref[j : j + 1, s * width : (s + 1) * width] for s in range(tasks)]
            + [jnp.zeros((gates - tasks, width), BF)],
            axis=0,
        )
        own.append(jax.nn.sigmoid(logits(gate)))
    total = values[0] + values[1] + own[0] + own[1]
    first = jnp.where(pick == 0, own[0], own[1])
    second = jnp.where(pick == 0, own[1], own[0])
    columns = [v / total for v in (values[0], values[1], first, second)] + [rows_ref[...]]
    high = sum(c.shape[0] for c in columns)
    full = -(-high // 128) * 128
    columns.append(jnp.zeros((full - high, count), F32))
    w_ref[...] = jnp.concatenate(columns, axis=0).T


def weights(me, pick, rows, sent, g0, g1, shared_gate, tasks, order):
    smem = pl.BlockSpec(memory_space=pltpu.SMEM)
    vmem = pl.BlockSpec(memory_space=pltpu.VMEM)
    gates = -(-tasks // PAD) * PAD
    full = -(-(4 * gates + rows.shape[0]) // 128) * 128
    return call(
        functools.partial(weight_kernel, tasks, order),
        jax.ShapeDtypeStruct((rows.shape[1], full), F32),
        in_specs=[smem, smem] + [vmem] * 5,
        out_specs=vmem,
        cost_estimate=cost(8 * sent.size * gates * len(order), 4 * g0.size + 2 * sent.size),
    )(me, pick, rows, sent, g0, g1, shared_gate)


def collect_kernel(chips, first, w_ref, *refs):
    ins, mine_ref, other_ref = refs[:chips], refs[-2], refs[-1]
    depth = ins[0].shape[0] // 2
    count = w_ref.shape[0]
    ids = lax.broadcasted_iota(I32, (count, chips * depth), 1).astype(F32)
    for side, out in ((0, mine_ref), (1, other_ref)):
        rows = jnp.concatenate([r[side * depth : (side + 1) * depth] for r in ins], axis=0)
        for k in range(2):
            column = first + 2 * side + k
            table = jnp.where(w_ref[:, column : column + 1] == ids, 1.0, 0.0).astype(BF)
            out[k * count : (k + 1) * count] = jnp.dot(
                table, rows, preferred_element_type=F32
            ).astype(BF)


def collect(w, blocks, first):
    vmem = pl.BlockSpec(memory_space=pltpu.VMEM)
    count, width = w.shape[0], blocks[0].shape[1]
    slots = sum(b.shape[0] for b in blocks)
    return call(
        functools.partial(collect_kernel, len(blocks), first),
        [jax.ShapeDtypeStruct((2 * count, width), BF)] * 2,
        in_specs=[vmem] * (1 + len(blocks)),
        out_specs=[vmem] * 2,
        cost_estimate=cost(4 * count * slots * width, 2 * slots * width + 8 * count * width),
    )(w, *blocks)


def mix_kernel(tasks, gates, w_ref, a0, a1, b0, b1, s0, s1, x_ref, out_ref):
    rows = [
        (a0[...] + b0[...]).astype(F32),
        (a1[...] + b1[...]).astype(F32),
        s0[...].astype(F32) + s1[...].astype(F32),
        x_ref[...].astype(F32),
    ]
    for s in range(tasks):
        mixed = None
        for j, row in enumerate(rows):
            column = j * gates + s
            term = w_ref[:, column : column + 1] * row
            mixed = term if mixed is None else mixed + term
        out_ref[s] = mixed.astype(BF)


def mix(w, mine, theirs, keep, back, far, tasks, block=64):
    count, full = w.shape
    width = far.shape[1]
    gates = -(-tasks // PAD) * PAD
    steps = count // block
    low = pl.BlockSpec((block, width), lambda i: (i, 0))
    high = pl.BlockSpec((block, width), lambda i: (i + steps, 0))
    return call(
        functools.partial(mix_kernel, tasks, gates),
        jax.ShapeDtypeStruct((tasks, count, width), BF),
        grid=(steps,),
        in_specs=[pl.BlockSpec((block, full), lambda i: (i, 0)), low, high, low, high, low, low, low],
        out_specs=pl.BlockSpec((tasks, block, width), lambda i: (0, i, 0)),
        cost_estimate=cost(8 * tasks * count * width, 2 * (tasks + 8) * count * width),
    )(w, mine, mine, theirs, theirs, keep, back, far)


def on_device(
    tokens, routes, capacity, expert_in, expert_out, shared_in, shared_out, route_gate, shared_gate
):
    experts = lax.axis_size("ep")
    chips = experts // 2
    count, width = tokens.shape
    tasks = shared_gate.shape[1] // width
    units = shared_in.shape[1]
    depth = max(4, 4 * count // experts)
    me = lax.axis_index("ep").astype(I32).reshape(1)
    pick = lax.axis_index("dp").astype(I32).reshape(1)

    def swap(x, mask):
        return lax.ppermute(x, "ep", [(i, i ^ mask) for i in range(experts)])

    def across(x):
        groups = lax.axis_size("dp")
        return lax.ppermute(x, "dp", [(i, groups - 1 - i) for i in range(groups)])

    half = chips // 2
    near = near_masks(chips)
    turned = routes.T
    packed, sent, limit = pack(
        me, pick, shared_in, shared_out, route_gate, tokens, turned, capacity, tasks
    )
    opposite = swap(sent, half * 2)
    partner = swap(sent, 1)
    opposite_partner = swap(opposite, 1)
    visitor = across(tokens)
    partner_visitor = swap(visitor, 1)

    shards = {0: packed}
    for q in range(1, chips):
        shards[q] = swap(shards[q & (q - 1)], 2 * (q & -q))

    *outgoing, rows = dispatch(me, limit, sent, partner, depth, 1)
    passing = dispatch(me, limit, opposite, opposite_partner, depth, 0)
    arrived = {0: outgoing[0], half: passing[0]}
    for m in near:
        arrived[m] = swap(outgoing[m], 2 * m)
        arrived[half + m] = swap(passing[m], 2 * m)

    w1, w2 = load(expert_in[0], expert_out[0])
    early, late = [0, half] + near, [half + m for m in near]
    results = dict(zip(early, expert(w1, w2, [arrived[m] for m in early])))
    results.update(zip(late, expert(w1, w2, [arrived[m] for m in late])))
    back = {0: results[0]}
    for m in early[1:] + late:
        back[m] = swap(results[m], 2 * m)

    samples = (sent, visitor, partner, partner_visitor)
    low, high = range(half), range(half, chips)
    part = shared([shards[q] for q in low], units, samples, count)
    keep, send = shared([shards[q] for q in high], units, samples, count, part)
    summed = swap(send, 1)
    crossing = (keep[count:].astype(F32) + summed[count : 2 * count].astype(F32)).astype(BF)
    far_rows = across(crossing)
    order = tuple(2 * q for q in range(chips))
    w = weights(me, pick, rows, sent, send, summed, shared_gate, tasks, order)
    mine, other = collect(w, [back[m] for m in range(chips)], 4 * (-(-tasks // PAD) * PAD))
    theirs = swap(other, 1)
    mixed = mix(w, mine, theirs, keep, summed, far_rows, tasks)
    return mixed.transpose(1, 0, 2)


def near_masks(chips):
    return list(range(chips // 2 - 1, 0, -1))


def solution(mesh):
    return jax.shard_map(
        on_device,
        mesh=mesh,
        in_specs=(
            P(("dp", "ep"), None),
            P(("dp", "ep"), None),
            P(),
            P("ep", None, None),
            P("ep", None, None),
            P(None, "ep", None),
            P(None, "ep", None),
            P("ep", None),
            P(),
        ),
        out_specs=P(("dp", "ep"), None, None),
        check_vma=False,
    )
```

profile of v0, /device:TPU:8, one launch (start us, length us, event | category | flops | bytes accessed | tf_op | source)
XLA Modules:
  0.0 103.4 jit_solution(16756802418509851491)
XLA Ops:
  1.1 2.7 %collective-permute-start.1 = (bf16[272,512]{1,0:T(8,128)(2,1)S(1)}, bf16[272,512]{1,0:T(8,128)(2,1)S(1)}, u32[]{:S(2)}, u32[]{:S(2)}) collective-permute-start(bf16[272,512]{1,0:T(8,128)(2,1)S(1)} %get-tuple-element.36.refs_0_), channel_id=1, source_target_pairs={{0,8},{1,9},{2,10},{3,11},{4,12},{5,13},{6,14},{7,15},{8,0},{9,1},... | collective-permute-start | bytes 835592 | tf_op jit(solution)/shard_map/ppermute | solution.py:413
  4.2 1.5 %collective-permute-start.5 = (bf16[256,512]{1,0:T(8,128)(2,1)}, bf16[256,512]{1,0:T(8,128)(2,1)S(1)}, u32[]{:S(2)}, u32[]{:S(2)}) collective-permute-start(bf16[256,512]{1,0:T(8,128)(2,1)} %refs_3_.1), channel_id=1, source_target_pairs={{0,16},{16,0},{1,17},{17,1},{2,18},{18,2},{3,19},{19,3},{4,20},{20... | collective-permute-start | bytes 786440 | tf_op jit(solution)/shard_map/ppermute | solution.py:417
  6.1 10.4 %collective-permute-done.1.refs_0_ = bf16[272,512]{1,0:T(8,128)(2,1)S(1)} collective-permute-done((bf16[272,512]{1,0:T(8,128)(2,1)S(1)}, bf16[272,512]{1,0:T(8,128)(2,1)S(1)}, u32[]{:S(2)}, u32[]{:S(2)}) %collective-permute-start.1) | collective-permute-done | bytes 278560 | tf_op jit(solution)/shard_map/ppermute | solution.py:413
  16.5 2.1 %collective-permute-start.3 = (bf16[272,512]{1,0:T(8,128)(2,1)S(1)}, bf16[272,512]{1,0:T(8,128)(2,1)S(1)}, u32[]{:S(2)}, u32[]{:S(2)}) collective-permute-start(bf16[272,512]{1,0:T(8,128)(2,1)S(1)} %collective-permute-done.1.refs_0_), channel_id=1, source_target_pairs={{0,4},{1,5},{2,6},{3,7},{4,0},{5,1},{6,2},{7,3},{8,12},{9,13},{10,... | collective-permute-start | bytes 835592 | tf_op jit(solution)/shard_map/ppermute | solution.py:413
  18.6 2.1 %collective-permute-start.7 = (bf16[272,512]{1,0:T(8,128)(2,1)S(1)}, bf16[272,512]{1,0:T(8,128)(2,1)S(1)}, u32[]{:S(2)}, u32[]{:S(2)}) collective-permute-start(bf16[272,512]{1,0:T(8,128)(2,1)S(1)} %get-tuple-element.36.refs_0_), channel_id=1, source_target_pairs={{0,2},{1,3},{2,0},{3,1},{4,6},{5,7},{6,4},{7,5},{8,10},{9,11},{10,... | collective-permute-start | bytes 835592 | tf_op jit(solution)/shard_map/ppermute | solution.py:413
  20.8 6.8 %collective-permute-done.11.t0_ref = bf16[272,512]{1,0:T(8,128)(2,1)S(1)} collective-permute-done((bf16[272,512]{1,0:T(8,128)(2,1)S(1)}, bf16[272,512]{1,0:T(8,128)(2,1)S(1)}, u32[]{:S(2)}, u32[]{:S(2)}) %collective-permute-start.11) | collective-permute-done | bytes 278560 | tf_op jit(solution)/shard_map/ppermute | solution.py:413
  27.6 1.5 %collective-permute-start.2 = (bf16[272,512]{1,0:T(8,128)(2,1)S(1)}, bf16[272,512]{1,0:T(8,128)(2,1)S(1)}, u32[]{:S(2)}, u32[]{:S(2)}) collective-permute-start(bf16[272,512]{1,0:T(8,128)(2,1)S(1)} %collective-permute-done.1.refs_0_), channel_id=1, source_target_pairs={{0,2},{1,3},{2,0},{3,1},{4,6},{5,7},{6,4},{7,5},{8,10},{9,11},{10,... | collective-permute-start | bytes 835592 | tf_op jit(solution)/shard_map/ppermute | solution.py:413
  32.1 5.0 %collective-permute-done.2.refs_1_ = bf16[272,512]{1,0:T(8,128)(2,1)S(1)} collective-permute-done((bf16[272,512]{1,0:T(8,128)(2,1)S(1)}, bf16[272,512]{1,0:T(8,128)(2,1)S(1)}, u32[]{:S(2)}, u32[]{:S(2)}) %collective-permute-start.2) | collective-permute-done | bytes 278560 | tf_op jit(solution)/shard_map/ppermute | solution.py:413
  37.1 5.5 %collective-permute-done.4.refs_3_ = bf16[272,512]{1,0:T(8,128)(2,1)S(1)} collective-permute-done((bf16[272,512]{1,0:T(8,128)(2,1)S(1)}, bf16[272,512]{1,0:T(8,128)(2,1)S(1)}, u32[]{:S(2)}, u32[]{:S(2)}) %collective-permute-start.4) | collective-permute-done | bytes 278560 | tf_op jit(solution)/shard_map/ppermute | solution.py:413
  44.7 2.7 %collective-permute-start.13 = (bf16[128,512]{1,0:T(8,128)(2,1)S(1)}, bf16[128,512]{1,0:T(8,128)(2,1)S(1)}, u32[]{:S(2)}, u32[]{:S(2)}) collective-permute-start(bf16[128,512]{1,0:T(8,128)(2,1)S(1)} %get-tuple-element.44), channel_id=1, source_target_pairs={{0,6},{1,7},{2,4},{3,5},{4,2},{5,3},{6,0},{7,1},{8,14},{9,15},{10,... | collective-permute-start | bytes 393224 | tf_op jit(solution)/shard_map/ppermute | solution.py:413
  48.3 2.2 %shard_map.96 = (bf16[512,2048]{1,0:T(8,128)(2,1)S(1)}, bf16[2048,512]{1,0:T(8,128)(2,1)S(1)}) custom-call(bf16[512,2048]{1,0:T(8,128)(2,1)} %bitcast.6, bf16[2048,512]{1,0:T(8,128)(2,1)} %bitcast.7), custom_call_target="tpu_custom_call" | custom-call | bytes 8388608 | tf_op jit(solution)/shard_map/pallas_call | solution.py:179
  51.1 2.7 %collective-permute-start.20 = (bf16[128,512]{1,0:T(8,128)(2,1)S(1)}, bf16[128,512]{1,0:T(8,128)(2,1)S(1)}, u32[]{:S(2)}, u32[]{:S(2)}) collective-permute-start(bf16[128,512]{1,0:T(8,128)(2,1)S(1)} %get-tuple-element.52), channel_id=1, source_target_pairs={{0,6},{1,7},{2,4},{3,5},{4,2},{5,3},{6,0},{7,1},{8,14},{9,15},{10,... | collective-permute-start | bytes 393224 | tf_op jit(solution)/shard_map/ppermute | solution.py:413
  55.3 3.7 %shard_map.98 = (bf16[128,512]{1,0:T(8,128)(2,1)S(1)}, bf16[128,512]{1,0:T(8,128)(2,1)S(1)}, bf16[128,512]{1,0:T(8,128)(2,1)S(1)}, bf16[128,512]{1,0:T(8,128)(2,1)S(1)}, bf16[128,512]{1,0:T(8,128)(2,1)S(1)}) custom-call(bf16[512,2048]{1,0:T(8,128)(2,1)S(1)} %get-tuple-element.40.w1_ref, bf16[2048,512]{1,0:T(8,128)(2,1)S(1)} %get-tuple-element.41.w2_ref, ...), custom_call_target="tpu_custom_call" | custom-call | flops 2684354560 | bytes 5505024 | tf_op jit(solution)/shard_map/pallas_call | solution.py:222
  60.4 1.8 %collective-permute-start.17 = (bf16[128,512]{1,0:T(8,128)(2,1)S(1)}, bf16[128,512]{1,0:T(8,128)(2,1)S(1)}, u32[]{:S(2)}, u32[]{:S(2)}) collective-permute-start(bf16[128,512]{1,0:T(8,128)(2,1)S(1)} %get-tuple-element.49), channel_id=1, source_target_pairs={{0,4},{1,5},{2,6},{3,7},{4,0},{5,1},{6,2},{7,3},{8,12},{9,13},{10,... | collective-permute-start | bytes 393224 | tf_op jit(solution)/shard_map/ppermute | solution.py:413
  62.6 3.9 %collective-permute-start.19 = (bf16[128,512]{1,0:T(8,128)(2,1)S(1)}, bf16[128,512]{1,0:T(8,128)(2,1)S(1)}, u32[]{:S(2)}, u32[]{:S(2)}) collective-permute-start(bf16[128,512]{1,0:T(8,128)(2,1)S(1)} %get-tuple-element.51), channel_id=1, source_target_pairs={{0,8},{1,9},{2,10},{3,11},{4,12},{5,13},{6,14},{7,15},{8,0},{9,1},... | collective-permute-start | bytes 393224 | tf_op jit(solution)/shard_map/ppermute | solution.py:413
  66.5 2.8 %shard_map.99 = (bf16[128,512]{1,0:T(8,128)(2,1)S(1)}, bf16[128,512]{1,0:T(8,128)(2,1)S(1)}, bf16[128,512]{1,0:T(8,128)(2,1)S(1)}) custom-call(bf16[512,2048]{1,0:T(8,128)(2,1)S(1)} %get-tuple-element.40.w1_ref, bf16[2048,512]{1,0:T(8,128)(2,1)S(1)} %get-tuple-element.41.w2_ref, bf16[128,512]{1,0:T(8,128)(2,1)S(1)} %collective-permute-done.20.refs_0_, ...), custom_call_target="tpu_custom_call" | custom-call | flops 1610612736 | bytes 4980736 | tf_op jit(solution)/shard_map/pallas_call | solution.py:222
  70.1 3.2 %collective-permute-start.24 = (bf16[128,512]{1,0:T(8,128)(2,1)S(1)}, bf16[128,512]{1,0:T(8,128)(2,1)S(1)}, u32[]{:S(2)}, u32[]{:S(2)}) collective-permute-start(bf16[128,512]{1,0:T(8,128)(2,1)S(1)} %get-tuple-element.56), channel_id=1, source_target_pairs={{0,12},{1,13},{2,14},{3,15},{4,8},{5,9},{6,10},{7,11},{8,4},{9,5},... | collective-permute-start | bytes 393224 | tf_op jit(solution)/shard_map/ppermute | solution.py:413
  73.9 6.4 %collective-permute-done.19.refs_4_ = bf16[128,512]{1,0:T(8,128)(2,1)S(1)} collective-permute-done((bf16[128,512]{1,0:T(8,128)(2,1)S(1)}, bf16[128,512]{1,0:T(8,128)(2,1)S(1)}, u32[]{:S(2)}, u32[]{:S(2)}) %collective-permute-start.19) | collective-permute-done | bytes 131104 | tf_op jit(solution)/shard_map/ppermute | solution.py:413
  80.3 2.8 %collective-permute-done.23.refs_5_ = bf16[128,512]{1,0:T(8,128)(2,1)S(1)} collective-permute-done((bf16[128,512]{1,0:T(8,128)(2,1)S(1)}, bf16[128,512]{1,0:T(8,128)(2,1)S(1)}, u32[]{:S(2)}, u32[]{:S(2)}) %collective-permute-start.23) | collective-permute-done | bytes 131104 | tf_op jit(solution)/shard_map/ppermute | solution.py:413
  83.1 5.1 %collective-permute-done.24.refs_6_ = bf16[128,512]{1,0:T(8,128)(2,1)S(1)} collective-permute-done((bf16[128,512]{1,0:T(8,128)(2,1)S(1)}, bf16[128,512]{1,0:T(8,128)(2,1)S(1)}, u32[]{:S(2)}, u32[]{:S(2)}) %collective-permute-start.24) | collective-permute-done | bytes 131104 | tf_op jit(solution)/shard_map/ppermute | solution.py:413
  88.2 2.1 %collective-permute-done.25.refs_7_ = bf16[128,512]{1,0:T(8,128)(2,1)S(1)} collective-permute-done((bf16[128,512]{1,0:T(8,128)(2,1)S(1)}, bf16[128,512]{1,0:T(8,128)(2,1)S(1)}, u32[]{:S(2)}, u32[]{:S(2)}) %collective-permute-start.25) | collective-permute-done | bytes 131104 | tf_op jit(solution)/shard_map/ppermute | solution.py:413
  91.2 1.6 %collective-permute-start.27 = (bf16[256,512]{1,0:T(8,128)(2,1)S(1)}, bf16[256,512]{1,0:T(8,128)(2,1)S(1)}, u32[]{:S(2)}, u32[]{:S(2)}) collective-permute-start(bf16[256,512]{1,0:T(8,128)(2,1)S(1)} %add_convert_fusion), channel_id=1, source_target_pairs={{0,16},{16,0},{1,17},{17,1},{2,18},{18,2},{3,19},{19,3},{4,20},{20... | collective-permute-start | bytes 786440 | tf_op jit(solution)/shard_map/ppermute | solution.py:417
  92.7 7.2 %collective-permute-done.27.x_ref = bf16[256,512]{1,0:T(8,128)(2,1)S(1)} collective-permute-done((bf16[256,512]{1,0:T(8,128)(2,1)S(1)}, bf16[256,512]{1,0:T(8,128)(2,1)S(1)}, u32[]{:S(2)}, u32[]{:S(2)}) %collective-permute-start.27) | collective-permute-done | bytes 262176 | tf_op jit(solution)/shard_map/ppermute | solution.py:417
  99.9 3.5 %shard_map.101 = bf16[12,256,512]{2,1,0:T(8,128)(2,1)} custom-call(f32[256,128]{1,0:T(8,128)S(1)} %shard_map.95.w_ref, bf16[512,512]{1,0:T(8,128)(2,1)S(1)} %get-tuple-element.58.a0.a1, bf16[512,512]{1,0:T(8,128)(2,1)S(1)} %get-tuple-element.58.a0.a1, bf16[512,512]{1,0:T(8,128)(2,1)S(1)} %collective-permute-done.26.b0.b1, ...), custom_call_target="tpu_custom_call" | custom-call | flops 12582912 | bytes 5242880 | tf_op jit(solution)/shard_map/pallas_call | solution.py:390
  (46 shorter events, 14.0 us)
Async XLA Ops:
  1.1 15.4 %collective-permute-start.1 = (bf16[272,512]{1,0:T(8,128)(2,1)S(1)}, bf16[272,512]{1,0:T(8,128)(2,1)S(1)}, u32[]{:S(2)}, u32[]{:S(2)}) collective-permute-start(bf16[272,512]{1,0:T(8,128)(2,1)S(1)} %get-tuple-element.36.refs_0_), channel_id=1, source_target_pairs={{0,8},{1,9},{2,10},{3,11},{4,12},{5,13},{6,14},{7,15},{8,0},{9,1},... | collective-permute-start | bytes 835592 | tf_op jit(solution)/shard_map/ppermute | solution.py:413
  3.8 16.9 %collective-permute-start.8 = (bf16[272,512]{1,0:T(8,128)(2,1)S(1)}, bf16[272,512]{1,0:T(8,128)(2,1)S(1)}, u32[]{:S(2)}, u32[]{:S(2)}) collective-permute-start(bf16[272,512]{1,0:T(8,128)(2,1)S(1)} %get-tuple-element.36.refs_0_), channel_id=1, source_target_pairs={{0,4},{1,5},{2,6},{3,7},{4,0},{5,1},{6,2},{7,3},{8,12},{9,13},{10,... | collective-permute-start | bytes 835592 | tf_op jit(solution)/shard_map/ppermute | solution.py:413
  4.2 14.4 %collective-permute-start.5 = (bf16[256,512]{1,0:T(8,128)(2,1)}, bf16[256,512]{1,0:T(8,128)(2,1)S(1)}, u32[]{:S(2)}, u32[]{:S(2)}) collective-permute-start(bf16[256,512]{1,0:T(8,128)(2,1)} %refs_3_.1), channel_id=1, source_target_pairs={{0,16},{16,0},{1,17},{17,1},{2,18},{18,2},{3,19},{19,3},{4,20},{20... | collective-permute-start | bytes 786440 | tf_op jit(solution)/shard_map/ppermute | solution.py:417
  5.7 21.8 %collective-permute-start.11 = (bf16[272,512]{1,0:T(8,128)(2,1)S(1)}, bf16[272,512]{1,0:T(8,128)(2,1)S(1)}, u32[]{:S(2)}, u32[]{:S(2)}) collective-permute-start(bf16[272,512]{1,0:T(8,128)(2,1)S(1)} %get-tuple-element.34.t0_ref.refs_4_.t_ref), channel_id=1, source_target_pairs={{0,8},{1,9},{2,10},{3,11},{4,12},{5,13},{6,14},{7,15},{8,0},{9,1},... | collective-permute-start | bytes 835592 | tf_op jit(solution)/shard_map/ppermute | solution.py:413
  6.1 21.5 %collective-permute-start = (bf16[272,512]{1,0:T(8,128)(2,1)S(1)}, bf16[272,512]{1,0:T(8,128)(2,1)S(1)}, u32[]{:S(2)}, u32[]{:S(2)}) collective-permute-start(bf16[272,512]{1,0:T(8,128)(2,1)S(1)} %get-tuple-element.34.t0_ref.refs_4_.t_ref), channel_id=1, source_target_pairs={{0,1},{1,0},{2,3},{3,2},{4,5},{5,4},{6,7},{7,6},{8,9},{9,8},{10,11... | collective-permute-start | bytes 835592 | tf_op jit(solution)/shard_map/ppermute | solution.py:413
  16.5 12.6 %collective-permute-start.3 = (bf16[272,512]{1,0:T(8,128)(2,1)S(1)}, bf16[272,512]{1,0:T(8,128)(2,1)S(1)}, u32[]{:S(2)}, u32[]{:S(2)}) collective-permute-start(bf16[272,512]{1,0:T(8,128)(2,1)S(1)} %collective-permute-done.1.refs_0_), channel_id=1, source_target_pairs={{0,4},{1,5},{2,6},{3,7},{4,0},{5,1},{6,2},{7,3},{8,12},{9,13},{10,... | collective-permute-start | bytes 835592 | tf_op jit(solution)/shard_map/ppermute | solution.py:413
  18.6 11.5 %collective-permute-start.7 = (bf16[272,512]{1,0:T(8,128)(2,1)S(1)}, bf16[272,512]{1,0:T(8,128)(2,1)S(1)}, u32[]{:S(2)}, u32[]{:S(2)}) collective-permute-start(bf16[272,512]{1,0:T(8,128)(2,1)S(1)} %get-tuple-element.36.refs_0_), channel_id=1, source_target_pairs={{0,2},{1,3},{2,0},{3,1},{4,6},{5,7},{6,4},{7,5},{8,10},{9,11},{10,... | collective-permute-start | bytes 835592 | tf_op jit(solution)/shard_map/ppermute | solution.py:413
  20.7 9.9 %collective-permute-start.9 = (bf16[272,512]{1,0:T(8,128)(2,1)S(1)}, bf16[272,512]{1,0:T(8,128)(2,1)S(1)}, u32[]{:S(2)}, u32[]{:S(2)}) collective-permute-start(bf16[272,512]{1,0:T(8,128)(2,1)S(1)} %collective-permute-done.8.refs_2_), channel_id=1, source_target_pairs={{0,2},{1,3},{2,0},{3,1},{4,6},{5,7},{6,4},{7,5},{8,10},{9,11},{10,... | collective-permute-start | bytes 835592 | tf_op jit(solution)/shard_map/ppermute | solution.py:413
  27.6 9.5 %collective-permute-start.2 = (bf16[272,512]{1,0:T(8,128)(2,1)S(1)}, bf16[272,512]{1,0:T(8,128)(2,1)S(1)}, u32[]{:S(2)}, u32[]{:S(2)}) collective-permute-start(bf16[272,512]{1,0:T(8,128)(2,1)S(1)} %collective-permute-done.1.refs_0_), channel_id=1, source_target_pairs={{0,2},{1,3},{2,0},{3,1},{4,6},{5,7},{6,4},{7,5},{8,10},{9,11},{10,... | collective-permute-start | bytes 835592 | tf_op jit(solution)/shard_map/ppermute | solution.py:413
  29.1 13.5 %collective-permute-start.4 = (bf16[272,512]{1,0:T(8,128)(2,1)S(1)}, bf16[272,512]{1,0:T(8,128)(2,1)S(1)}, u32[]{:S(2)}, u32[]{:S(2)}) collective-permute-start(bf16[272,512]{1,0:T(8,128)(2,1)S(1)} %collective-permute-done.3.refs_2_), channel_id=1, source_target_pairs={{0,2},{1,3},{2,0},{3,1},{4,6},{5,7},{6,4},{7,5},{8,10},{9,11},{10,... | collective-permute-start | bytes 835592 | tf_op jit(solution)/shard_map/ppermute | solution.py:413
  30.1 20.4 %collective-permute-start.12 = (bf16[272,512]{1,0:T(8,128)(2,1)S(1)}, bf16[272,512]{1,0:T(8,128)(2,1)S(1)}, u32[]{:S(2)}, u32[]{:S(2)}) collective-permute-start(bf16[272,512]{1,0:T(8,128)(2,1)S(1)} %collective-permute-done.11.t0_ref), channel_id=1, source_target_pairs={{0,1},{1,0},{2,3},{3,2},{4,5},{5,4},{6,7},{7,6},{8,9},{9,8},{10,11... | collective-permute-start | bytes 835592 | tf_op jit(solution)/shard_map/ppermute | solution.py:413
  44.1 29.3 %collective-permute-start.10 = (bf16[640,512]{1,0:T(8,128)(2,1)S(1)}, bf16[640,512]{1,0:T(8,128)(2,1)S(1)}, u32[]{:S(2)}, u32[]{:S(2)}) collective-permute-start(bf16[640,512]{1,0:T(8,128)(2,1)S(1)} %get-tuple-element.39.g0_ref), channel_id=1, source_target_pairs={{0,1},{1,0},{2,3},{3,2},{4,5},{5,4},{6,7},{7,6},{8,9},{9,8},{10,11... | collective-permute-start | bytes 1966088 | tf_op jit(solution)/shard_map/ppermute | solution.py:413
  44.7 9.1 %collective-permute-start.13 = (bf16[128,512]{1,0:T(8,128)(2,1)S(1)}, bf16[128,512]{1,0:T(8,128)(2,1)S(1)}, u32[]{:S(2)}, u32[]{:S(2)}) collective-permute-start(bf16[128,512]{1,0:T(8,128)(2,1)S(1)} %get-tuple-element.44), channel_id=1, source_target_pairs={{0,6},{1,7},{2,4},{3,5},{4,2},{5,3},{6,0},{7,1},{8,14},{9,15},{10,... | collective-permute-start | bytes 393224 | tf_op jit(solution)/shard_map/ppermute | solution.py:413
  51.1 9.4 %collective-permute-start.20 = (bf16[128,512]{1,0:T(8,128)(2,1)S(1)}, bf16[128,512]{1,0:T(8,128)(2,1)S(1)}, u32[]{:S(2)}, u32[]{:S(2)}) collective-permute-start(bf16[128,512]{1,0:T(8,128)(2,1)S(1)} %get-tuple-element.52), channel_id=1, source_target_pairs={{0,6},{1,7},{2,4},{3,5},{4,2},{5,3},{6,0},{7,1},{8,14},{9,15},{10,... | collective-permute-start | bytes 393224 | tf_op jit(solution)/shard_map/ppermute | solution.py:413
  53.8 8.4 %collective-permute-start.21 = (bf16[128,512]{1,0:T(8,128)(2,1)S(1)}, bf16[128,512]{1,0:T(8,128)(2,1)S(1)}, u32[]{:S(2)}, u32[]{:S(2)}) collective-permute-start(bf16[128,512]{1,0:T(8,128)(2,1)S(1)} %get-tuple-element.53), channel_id=1, source_target_pairs={{0,4},{1,5},{2,6},{3,7},{4,0},{5,1},{6,2},{7,3},{8,12},{9,13},{10,... | collective-permute-start | bytes 393224 | tf_op jit(solution)/shard_map/ppermute | solution.py:413
  59.1 10.3 %collective-permute-start.16 = (bf16[128,512]{1,0:T(8,128)(2,1)S(1)}, bf16[128,512]{1,0:T(8,128)(2,1)S(1)}, u32[]{:S(2)}, u32[]{:S(2)}) collective-permute-start(bf16[128,512]{1,0:T(8,128)(2,1)S(1)} %get-tuple-element.48), channel_id=1, source_target_pairs={{0,2},{1,3},{2,0},{3,1},{4,6},{5,7},{6,4},{7,5},{8,10},{9,11},{10,... | collective-permute-start | bytes 393224 | tf_op jit(solution)/shard_map/ppermute | solution.py:413
  60.4 9.7 %collective-permute-start.17 = (bf16[128,512]{1,0:T(8,128)(2,1)S(1)}, bf16[128,512]{1,0:T(8,128)(2,1)S(1)}, u32[]{:S(2)}, u32[]{:S(2)}) collective-permute-start(bf16[128,512]{1,0:T(8,128)(2,1)S(1)} %get-tuple-element.49), channel_id=1, source_target_pairs={{0,4},{1,5},{2,6},{3,7},{4,0},{5,1},{6,2},{7,3},{8,12},{9,13},{10,... | collective-permute-start | bytes 393224 | tf_op jit(solution)/shard_map/ppermute | solution.py:413
  62.2 11.7 %collective-permute-start.18 = (bf16[128,512]{1,0:T(8,128)(2,1)S(1)}, bf16[128,512]{1,0:T(8,128)(2,1)S(1)}, u32[]{:S(2)}, u32[]{:S(2)}) collective-permute-start(bf16[128,512]{1,0:T(8,128)(2,1)S(1)} %get-tuple-element.50), channel_id=1, source_target_pairs={{0,6},{1,7},{2,4},{3,5},{4,2},{5,3},{6,0},{7,1},{8,14},{9,15},{10,... | collective-permute-start | bytes 393224 | tf_op jit(solution)/shard_map/ppermute | solution.py:413
  62.6 17.6 %collective-permute-start.19 = (bf16[128,512]{1,0:T(8,128)(2,1)S(1)}, bf16[128,512]{1,0:T(8,128)(2,1)S(1)}, u32[]{:S(2)}, u32[]{:S(2)}) collective-permute-start(bf16[128,512]{1,0:T(8,128)(2,1)S(1)} %get-tuple-element.51), channel_id=1, source_target_pairs={{0,8},{1,9},{2,10},{3,11},{4,12},{5,13},{6,14},{7,15},{8,0},{9,1},... | collective-permute-start | bytes 393224 | tf_op jit(solution)/shard_map/ppermute | solution.py:413
  69.3 13.8 %collective-permute-start.23 = (bf16[128,512]{1,0:T(8,128)(2,1)S(1)}, bf16[128,512]{1,0:T(8,128)(2,1)S(1)}, u32[]{:S(2)}, u32[]{:S(2)}) collective-permute-start(bf16[128,512]{1,0:T(8,128)(2,1)S(1)} %get-tuple-element.55), channel_id=1, source_target_pairs={{0,10},{1,11},{2,8},{3,9},{4,14},{5,15},{6,12},{7,13},{8,2},{9,3},... | collective-permute-start | bytes 393224 | tf_op jit(solution)/shard_map/ppermute | solution.py:413
  70.1 18.0 %collective-permute-start.24 = (bf16[128,512]{1,0:T(8,128)(2,1)S(1)}, bf16[128,512]{1,0:T(8,128)(2,1)S(1)}, u32[]{:S(2)}, u32[]{:S(2)}) collective-permute-start(bf16[128,512]{1,0:T(8,128)(2,1)S(1)} %get-tuple-element.56), channel_id=1, source_target_pairs={{0,12},{1,13},{2,14},{3,15},{4,8},{5,9},{6,10},{7,11},{8,4},{9,5},... | collective-permute-start | bytes 393224 | tf_op jit(solution)/shard_map/ppermute | solution.py:413
  73.4 16.9 %collective-permute-start.25 = (bf16[128,512]{1,0:T(8,128)(2,1)S(1)}, bf16[128,512]{1,0:T(8,128)(2,1)S(1)}, u32[]{:S(2)}, u32[]{:S(2)}) collective-permute-start(bf16[128,512]{1,0:T(8,128)(2,1)S(1)} %get-tuple-element.57), channel_id=1, source_target_pairs={{0,14},{1,15},{2,12},{3,13},{4,10},{5,11},{6,8},{7,9},{8,6},{9,7},... | collective-permute-start | bytes 393224 | tf_op jit(solution)/shard_map/ppermute | solution.py:413
  91.0 8.9 %collective-permute-start.26 = (bf16[512,512]{1,0:T(8,128)(2,1)S(1)}, bf16[512,512]{1,0:T(8,128)(2,1)S(1)}, u32[]{:S(2)}, u32[]{:S(2)}) collective-permute-start(bf16[512,512]{1,0:T(8,128)(2,1)S(1)} %get-tuple-element.59), channel_id=1, source_target_pairs={{0,1},{1,0},{2,3},{3,2},{4,5},{5,4},{6,7},{7,6},{8,9},{9,8},{10,11... | collective-permute-start | bytes 1572872 | tf_op jit(solution)/shard_map/ppermute | solution.py:413
  91.2 8.8 %collective-permute-start.27 = (bf16[256,512]{1,0:T(8,128)(2,1)S(1)}, bf16[256,512]{1,0:T(8,128)(2,1)S(1)}, u32[]{:S(2)}, u32[]{:S(2)}) collective-permute-start(bf16[256,512]{1,0:T(8,128)(2,1)S(1)} %add_convert_fusion), channel_id=1, source_target_pairs={{0,16},{16,0},{1,17},{17,1},{2,18},{18,2},{3,19},{19,3},{4,20},{20... | collective-permute-start | bytes 786440 | tf_op jit(solution)/shard_map/ppermute | solution.py:417
  (5 other events, 36.1 us)
where the time goes:
time: 104 us; the launch traced here: 103 us
  waiting for transfers between devices  52.3 us (50%)
  starting transfers between devices  32.2 us (31%)
  Pallas kernels  18.7 us (18%)
    ppermute x26, waiting for transfers between devices, swap(): return lax.ppermute(x, 'ep', [(i, i ^ mask) for i in range(experts)])  45.1 us
    ppermute x26, starting transfers between devices, swap(): return lax.ppermute(x, 'ep', [(i, i ^ mask) for i in range(experts)])  29.2 us
    ppermute x2, waiting for transfers between devices, across(): return lax.ppermute(x, 'dp', [(i, groups - 1 - i) for i in range(groups)])  7.22 us
    pallas_call x2, Pallas kernels, expert(): call(functools.partial(expert_kernel, len(xs)), [jax.ShapeDtypeStruct((ro...  6.56 us
    pallas_call x1, Pallas kernels, mix(): call(functools.partial(mix_kernel, tasks, gates), jax.ShapeDtypeStruct((t...  3.47 us
    ppermute x2, starting transfers between devices, across(): return lax.ppermute(x, 'dp', [(i, groups - 1 - i) for i in range(groups)])  3.05 us
    pallas_call x2, Pallas kernels, shared(): call(functools.partial(shared_kernel, len(shards), units, bool(carried),...  2.95 us
    pallas_call x1, Pallas kernels, load(): call(load_kernel, [jax.ShapeDtypeStruct(a.shape, a.dtype), jax.ShapeDtype...  2.21 us
  transfers between devices with their start and end apart: 28, of which 11 were waited for; matrix products, arithmetic and copies ran while one was open for 0% of the time, Pallas kernels for 13%

commit v1 on v0

--- a/solution.py
+++ b/solution.py
@@ -234,13 +234,13 @@
     )(w1, w2, *xs)
 
 
-def shared_kernel(shards, units, last, group, *refs):
-    ins, tokens, refs = refs[:shards], refs[shards : shards + 4], refs[shards + 4 :]
-    rows = refs[-1].shape[0] // 4
-    count = rows
+def shared_kernel(shards, units, group, start, gated, count, *refs):
+    ins, refs = refs[:shards], refs[shards:]
     x_ref = refs[-1]
-    for i, t in enumerate(tokens):
-        x_ref[i * rows : (i + 1) * rows] = t[0:count]
+    blocks = x_ref.shape[0] // count
+    for i in range(blocks):
+        x_ref[i * count : (i + 1) * count] = refs[i][0:count]
+    refs = refs[blocks:-1]
     total = None
     for first in range(0, shards, group):
         part = ins[first : first + group]
@@ -249,36 +249,37 @@
         hidden = jax.nn.gelu(dot_t(x_ref[...], up)).astype(BF)
         term = jnp.dot(hidden, down, preferred_element_type=F32)
         total = term if total is None else total + term
-    gates = jnp.concatenate([w[2 * units :] for w in ins], axis=0)
-    if last:
-        before, early, keep_ref, send_ref = refs[:4]
-        total = total + before[...]
-        keep_ref[...] = total[0 : 2 * rows].astype(BF)
-        send_ref[0 : 2 * rows] = total[2 * rows :].astype(BF)
-        send_ref[2 * rows : 2 * rows + gates.shape[0]] = early[...]
-        send_ref[2 * rows + gates.shape[0] :] = gates
-    else:
+    if start is None:
         refs[0][...] = total
-        refs[1][...] = gates
-
-
-def shared(shards, units, tokens, count, carried=()):
+        refs[1][...] = jnp.concatenate([w[2 * units :] for w in ins], axis=0)
+        return
+    before, early, keep_ref, send_ref = refs
+    total = total + before[start : start + blocks * count]
+    keep_ref[...] = total[0:count].astype(BF)
+    send_ref[0:count] = total[count:].astype(BF)
+    if gated:
+        gates = jnp.concatenate([early[...]] + [w[2 * units :] for w in ins], axis=0)
+        send_ref[count:] = gates
+
+
+def shared(shards, units, tokens, count, carried=(), start=None, gated=False):
     width = shards[0].shape[1]
     gates = len(shards) * (shards[0].shape[0] - 2 * units)
     vmem = pl.BlockSpec(memory_space=pltpu.VMEM)
     if carried:
-        shapes = [((2 * count, width), BF), ((2 * count + 2 * gates, width), BF)]
+        extra = 2 * gates if gated else 0
+        shapes = [((count, width), BF), ((count + extra, width), BF)]
     else:
-        shapes = [((4 * count, width), F32), ((gates, width), BF)]
+        shapes = [((len(tokens) * count, width), F32), ((gates, width), BF)]
     group = max(1, min(len(shards), 256 // units))
     return call(
-        functools.partial(shared_kernel, len(shards), units, bool(carried), group),
+        functools.partial(shared_kernel, len(shards), units, group, start, gated, count),
         [jax.ShapeDtypeStruct(*shape) for shape in shapes],
-        in_specs=[vmem] * (len(shards) + 4 + len(carried)),
+        in_specs=[vmem] * (len(shards) + len(tokens) + len(carried)),
         out_specs=[vmem] * 2,
-        scratch_shapes=[pltpu.VMEM((4 * count, width), BF)],
+        scratch_shapes=[pltpu.VMEM((len(tokens) * count, width), BF)],
         cost_estimate=cost(
-            16 * count * width * units * len(shards), 4 * len(shards) * units * width
+            4 * len(tokens) * count * width * units * len(shards), 4 * len(shards) * units * width
         ),
     )(*shards, *tokens, *carried)
 
@@ -447,12 +448,15 @@
     for m in early[1:] + late:
         back[m] = swap(results[m], 2 * m)
 
-    samples = (sent, visitor, partner, partner_visitor)
-    low, high = range(half), range(half, chips)
-    part = shared([shards[q] for q in low], units, samples, count)
-    keep, send = shared([shards[q] for q in high], units, samples, count, part)
+    guests, own = (visitor, partner_visitor), (sent, partner)
+    low = [shards[q] for q in range(half)]
+    high = [shards[q] for q in range(half, chips)]
+    part = shared(low, units, guests + own, count)
+    guest_keep, guest_send = shared(high, units, guests, count, part, 0)
+    keep, send = shared(high, units, own, count, part, 2 * count, True)
+    guest_summed = swap(guest_send, 1)
     summed = swap(send, 1)
-    crossing = (keep[count:].astype(F32) + summed[count : 2 * count].astype(F32)).astype(BF)
+    crossing = (guest_keep.astype(F32) + guest_summed.astype(F32)).astype(BF)
     far_rows = across(crossing)
     order = tuple(2 * q for q in range(chips))
     w = weights(me, pick, rows, sent, send, summed, shared_gate, tasks, order)

time: 104 us -> 116 us (1.12)
  the two profiles are of different devices: /device:TPU:8 before, /device:TPU:18 now
where the time goes in v1:
time: 116 us
  waiting for transfers between devices  59.4 us (51%)
  starting transfers between devices  37 us (32%)
  Pallas kernels  19.1 us (16%)
    ppermute x27, waiting for transfers between devices, swap(): return lax.ppermute(x, 'ep', [(i, i ^ mask) for i in range(experts)])  51.2 us
    ppermute x27, starting transfers between devices, swap(): return lax.ppermute(x, 'ep', [(i, i ^ mask) for i in range(experts)])  35.9 us
    ppermute x2, waiting for transfers between devices, across(): return lax.ppermute(x, 'dp', [(i, groups - 1 - i) for i in range(groups)])  8.21 us
    pallas_call x2, Pallas kernels, expert(): call(functools.partial(expert_kernel, len(xs)), [jax.ShapeDtypeStruct((ro...  6.56 us
    pallas_call x1, Pallas kernels, mix(): call(functools.partial(mix_kernel, tasks, gates), jax.ShapeDtypeStruct((t...  3.48 us
    pallas_call x3, Pallas kernels, shared(): call(functools.partial(shared_kernel, len(shards), units, group, start, g...  3.31 us
  transfers between devices with their start and end apart: 29, of which 12 were waited for; matrix products, arithmetic and copies ran while one was open for 0% of the time, Pallas kernels for 13%

profile of v1, /device:TPU:18, one launch (start us, length us, event | category | flops | bytes accessed | tf_op | source)
XLA Modules:
  0.0 115.7 jit_solution(4489388152776101744)
XLA Ops:
  1.5 2.6 %collective-permute-start.11 = (bf16[272,512]{1,0:T(8,128)(2,1)S(1)}, bf16[272,512]{1,0:T(8,128)(2,1)S(1)}, u32[]{:S(2)}, u32[]{:S(2)}) collective-permute-start(bf16[272,512]{1,0:T(8,128)(2,1)S(1)} %get-tuple-element.36.t0_ref.refs_6_.refs_4_.t_ref), channel_id=1, source_target_pairs={{0,8},{1,9},{2,10},{3,11},{4,12},{5,13},{6,14},{7,15},{8,0},{9,1},... | collective-permute-start | bytes 835592 | tf_op jit(solution)/shard_map/ppermute | solution.py:414
  4.1 1.6 %collective-permute-start.6 = (bf16[272,512]{1,0:T(8,128)(2,1)S(1)}, bf16[272,512]{1,0:T(8,128)(2,1)S(1)}, u32[]{:S(2)}, u32[]{:S(2)}) collective-permute-start(bf16[272,512]{1,0:T(8,128)(2,1)S(1)} %get-tuple-element.38.refs_0_), channel_id=1, source_target_pairs={{0,4},{1,5},{2,6},{3,7},{4,0},{5,1},{6,2},{7,3},{8,12},{9,13},{10,... | collective-permute-start | bytes 835592 | tf_op jit(solution)/shard_map/ppermute | solution.py:414
  6.2 14.3 %collective-permute-done.1.refs_0_ = bf16[272,512]{1,0:T(8,128)(2,1)S(1)} collective-permute-done((bf16[272,512]{1,0:T(8,128)(2,1)S(1)}, bf16[272,512]{1,0:T(8,128)(2,1)S(1)}, u32[]{:S(2)}, u32[]{:S(2)}) %collective-permute-start.1) | collective-permute-done | bytes 278560 | tf_op jit(solution)/shard_map/ppermute | solution.py:414
  20.5 3.5 %collective-permute-start.3 = (bf16[272,512]{1,0:T(8,128)(2,1)S(1)}, bf16[272,512]{1,0:T(8,128)(2,1)S(1)}, u32[]{:S(2)}, u32[]{:S(2)}) collective-permute-start(bf16[272,512]{1,0:T(8,128)(2,1)S(1)} %collective-permute-done.1.refs_0_), channel_id=1, source_target_pairs={{0,4},{1,5},{2,6},{3,7},{4,0},{5,1},{6,2},{7,3},{8,12},{9,13},{10,... | collective-permute-start | bytes 835592 | tf_op jit(solution)/shard_map/ppermute | solution.py:414
  25.4 1.5 %collective-permute-start.5 = (bf16[272,512]{1,0:T(8,128)(2,1)S(1)}, bf16[272,512]{1,0:T(8,128)(2,1)S(1)}, u32[]{:S(2)}, u32[]{:S(2)}) collective-permute-start(bf16[272,512]{1,0:T(8,128)(2,1)S(1)} %get-tuple-element.38.refs_0_), channel_id=1, source_target_pairs={{0,2},{1,3},{2,0},{3,1},{4,6},{5,7},{6,4},{7,5},{8,10},{9,11},{10,... | collective-permute-start | bytes 835592 | tf_op jit(solution)/shard_map/ppermute | solution.py:414
  27.4 5.9 %collective-permute-done.3.refs_2_ = bf16[272,512]{1,0:T(8,128)(2,1)S(1)} collective-permute-done((bf16[272,512]{1,0:T(8,128)(2,1)S(1)}, bf16[272,512]{1,0:T(8,128)(2,1)S(1)}, u32[]{:S(2)}, u32[]{:S(2)}) %collective-permute-start.3) | collective-permute-done | bytes 278560 | tf_op jit(solution)/shard_map/ppermute | solution.py:414
  35.4 2.2 %shard_map.96 = (bf16[512,2048]{1,0:T(8,128)(2,1)S(1)}, bf16[2048,512]{1,0:T(8,128)(2,1)S(1)}) custom-call(bf16[512,2048]{1,0:T(8,128)(2,1)} %bitcast.6, bf16[2048,512]{1,0:T(8,128)(2,1)} %bitcast.7), custom_call_target="tpu_custom_call" | custom-call | bytes 8388608 | tf_op jit(solution)/shard_map/pallas_call | solution.py:179
  38.8 3.5 %collective-permute-start.13 = (bf16[128,512]{1,0:T(8,128)(2,1)S(1)}, bf16[128,512]{1,0:T(8,128)(2,1)S(1)}, u32[]{:S(2)}, u32[]{:S(2)}) collective-permute-start(bf16[128,512]{1,0:T(8,128)(2,1)S(1)} %get-tuple-element.46), channel_id=1, source_target_pairs={{0,6},{1,7},{2,4},{3,5},{4,2},{5,3},{6,0},{7,1},{8,14},{9,15},{10,... | collective-permute-start | bytes 393224 | tf_op jit(solution)/shard_map/ppermute | solution.py:414
  44.4 5.3 %collective-permute-done.2.refs_1_ = bf16[272,512]{1,0:T(8,128)(2,1)S(1)} collective-permute-done((bf16[272,512]{1,0:T(8,128)(2,1)S(1)}, bf16[272,512]{1,0:T(8,128)(2,1)S(1)}, u32[]{:S(2)}, u32[]{:S(2)}) %collective-permute-start.2) | collective-permute-done | bytes 278560 | tf_op jit(solution)/shard_map/ppermute | solution.py:414
  49.7 5.5 %collective-permute-start.20 = (bf16[128,512]{1,0:T(8,128)(2,1)S(1)}, bf16[128,512]{1,0:T(8,128)(2,1)S(1)}, u32[]{:S(2)}, u32[]{:S(2)}) collective-permute-start(bf16[128,512]{1,0:T(8,128)(2,1)S(1)} %get-tuple-element.54), channel_id=1, source_target_pairs={{0,6},{1,7},{2,4},{3,5},{4,2},{5,3},{6,0},{7,1},{8,14},{9,15},{10,... | collective-permute-start | bytes 393224 | tf_op jit(solution)/shard_map/ppermute | solution.py:414
  55.2 3.3 %collective-permute-done.4.refs_3_ = bf16[272,512]{1,0:T(8,128)(2,1)S(1)} collective-permute-done((bf16[272,512]{1,0:T(8,128)(2,1)S(1)}, bf16[272,512]{1,0:T(8,128)(2,1)S(1)}, u32[]{:S(2)}, u32[]{:S(2)}) %collective-permute-start.4) | collective-permute-done | bytes 278560 | tf_op jit(solution)/shard_map/ppermute | solution.py:414
  58.5 4.6 %collective-permute-start.21 = (bf16[128,512]{1,0:T(8,128)(2,1)S(1)}, bf16[128,512]{1,0:T(8,128)(2,1)S(1)}, u32[]{:S(2)}, u32[]{:S(2)}) collective-permute-start(bf16[128,512]{1,0:T(8,128)(2,1)S(1)} %get-tuple-element.55), channel_id=1, source_target_pairs={{0,4},{1,5},{2,6},{3,7},{4,0},{5,1},{6,2},{7,3},{8,12},{9,13},{10,... | collective-permute-start | bytes 393224 | tf_op jit(solution)/shard_map/ppermute | solution.py:414
  64.0 1.6 %collective-permute-start.22 = (bf16[128,512]{1,0:T(8,128)(2,1)S(1)}, bf16[128,512]{1,0:T(8,128)(2,1)S(1)}, u32[]{:S(2)}, u32[]{:S(2)}) collective-permute-start(bf16[128,512]{1,0:T(8,128)(2,1)S(1)} %get-tuple-element.56), channel_id=1, source_target_pairs={{0,2},{1,3},{2,0},{3,1},{4,6},{5,7},{6,4},{7,5},{8,10},{9,11},{10,... | collective-permute-start | bytes 393224 | tf_op jit(solution)/shard_map/ppermute | solution.py:414
  65.6 3.7 %shard_map.98 = (bf16[128,512]{1,0:T(8,128)(2,1)S(1)}, bf16[128,512]{1,0:T(8,128)(2,1)S(1)}, bf16[128,512]{1,0:T(8,128)(2,1)S(1)}, bf16[128,512]{1,0:T(8,128)(2,1)S(1)}, bf16[128,512]{1,0:T(8,128)(2,1)S(1)}) custom-call(bf16[512,2048]{1,0:T(8,128)(2,1)S(1)} %get-tuple-element.42.w1_ref, bf16[2048,512]{1,0:T(8,128)(2,1)S(1)} %get-tuple-element.43.w2_ref, ...), custom_call_target="tpu_custom_call" | custom-call | flops 2684354560 | bytes 5505024 | tf_op jit(solution)/shard_map/pallas_call | solution.py:222
  71.7 2.2 %collective-permute-start.18 = (bf16[128,512]{1,0:T(8,128)(2,1)S(1)}, bf16[128,512]{1,0:T(8,128)(2,1)S(1)}, u32[]{:S(2)}, u32[]{:S(2)}) collective-permute-start(bf16[128,512]{1,0:T(8,128)(2,1)S(1)} %get-tuple-element.52), channel_id=1, source_target_pairs={{0,6},{1,7},{2,4},{3,5},{4,2},{5,3},{6,0},{7,1},{8,14},{9,15},{10,... | collective-permute-start | bytes 393224 | tf_op jit(solution)/shard_map/ppermute | solution.py:414
  73.9 2.8 %shard_map.99 = (bf16[128,512]{1,0:T(8,128)(2,1)S(1)}, bf16[128,512]{1,0:T(8,128)(2,1)S(1)}, bf16[128,512]{1,0:T(8,128)(2,1)S(1)}) custom-call(bf16[512,2048]{1,0:T(8,128)(2,1)S(1)} %get-tuple-element.42.w1_ref, bf16[2048,512]{1,0:T(8,128)(2,1)S(1)} %get-tuple-element.43.w2_ref, bf16[128,512]{1,0:T(8,128)(2,1)S(1)} %collective-permute-done.20.refs_0_, ...), custom_call_target="tpu_custom_call" | custom-call | flops 1610612736 | bytes 4980736 | tf_op jit(solution)/shard_map/pallas_call | solution.py:222
  77.2 2.4 %collective-permute-start.23 = (bf16[128,512]{1,0:T(8,128)(2,1)S(1)}, bf16[128,512]{1,0:T(8,128)(2,1)S(1)}, u32[]{:S(2)}, u32[]{:S(2)}) collective-permute-start(bf16[128,512]{1,0:T(8,128)(2,1)S(1)} %get-tuple-element.57), channel_id=1, source_target_pairs={{0,10},{1,11},{2,8},{3,9},{4,14},{5,15},{6,12},{7,13},{8,2},{9,3},... | collective-permute-start | bytes 393224 | tf_op jit(solution)/shard_map/ppermute | solution.py:414
  81.0 1.8 %collective-permute-start.25 = (bf16[128,512]{1,0:T(8,128)(2,1)S(1)}, bf16[128,512]{1,0:T(8,128)(2,1)S(1)}, u32[]{:S(2)}, u32[]{:S(2)}) collective-permute-start(bf16[128,512]{1,0:T(8,128)(2,1)S(1)} %get-tuple-element.59), channel_id=1, source_target_pairs={{0,14},{1,15},{2,12},{3,13},{4,10},{5,11},{6,8},{7,9},{8,6},{9,7},... | collective-permute-start | bytes 393224 | tf_op jit(solution)/shard_map/ppermute | solution.py:414
  83.3 8.5 %collective-permute-done.19.refs_4_ = bf16[128,512]{1,0:T(8,128)(2,1)S(1)} collective-permute-done((bf16[128,512]{1,0:T(8,128)(2,1)S(1)}, bf16[128,512]{1,0:T(8,128)(2,1)S(1)}, u32[]{:S(2)}, u32[]{:S(2)}) %collective-permute-start.19) | collective-permute-done | bytes 131104 | tf_op jit(solution)/shard_map/ppermute | solution.py:414
  91.8 2.8 %collective-permute-done.23.refs_5_ = bf16[128,512]{1,0:T(8,128)(2,1)S(1)} collective-permute-done((bf16[128,512]{1,0:T(8,128)(2,1)S(1)}, bf16[128,512]{1,0:T(8,128)(2,1)S(1)}, u32[]{:S(2)}, u32[]{:S(2)}) %collective-permute-start.23) | collective-permute-done | bytes 131104 | tf_op jit(solution)/shard_map/ppermute | solution.py:414
  94.6 4.9 %collective-permute-done.24.refs_6_ = bf16[128,512]{1,0:T(8,128)(2,1)S(1)} collective-permute-done((bf16[128,512]{1,0:T(8,128)(2,1)S(1)}, bf16[128,512]{1,0:T(8,128)(2,1)S(1)}, u32[]{:S(2)}, u32[]{:S(2)}) %collective-permute-start.24) | collective-permute-done | bytes 131104 | tf_op jit(solution)/shard_map/ppermute | solution.py:414
  99.5 3.0 %collective-permute-done.25.refs_7_ = bf16[128,512]{1,0:T(8,128)(2,1)S(1)} collective-permute-done((bf16[128,512]{1,0:T(8,128)(2,1)S(1)}, bf16[128,512]{1,0:T(8,128)(2,1)S(1)}, u32[]{:S(2)}, u32[]{:S(2)}) %collective-permute-start.25) | collective-permute-done | bytes 131104 | tf_op jit(solution)/shard_map/ppermute | solution.py:414
  104.0 8.2 %collective-permute-done.28.x_ref = bf16[256,512]{1,0:T(8,128)(2,1)S(1)} collective-permute-done((bf16[256,512]{1,0:T(8,128)(2,1)S(1)}, bf16[256,512]{1,0:T(8,128)(2,1)S(1)}, u32[]{:S(2)}, u32[]{:S(2)}) %collective-permute-start.28) | collective-permute-done | bytes 262176 | tf_op jit(solution)/shard_map/ppermute | solution.py:418
  112.2 3.5 %shard_map.102 = bf16[12,256,512]{2,1,0:T(8,128)(2,1)} custom-call(f32[256,128]{1,0:T(8,128)S(1)} %shard_map.95.w_ref, bf16[512,512]{1,0:T(8,128)(2,1)S(1)} %get-tuple-element.60.a0.a1, bf16[512,512]{1,0:T(8,128)(2,1)S(1)} %get-tuple-element.60.a0.a1, bf16[512,512]{1,0:T(8,128)(2,1)S(1)} %collective-permute-done.26.b0.b1, ...), custom_call_target="tpu_custom_call" | custom-call | flops 12582912 | bytes 5242880 | tf_op jit(solution)/shard_map/pallas_call | solution.py:391
  (49 shorter events, 16.5 us)
Async XLA Ops:
  1.1 19.4 %collective-permute-start.1 = (bf16[272,512]{1,0:T(8,128)(2,1)S(1)}, bf16[272,512]{1,0:T(8,128)(2,1)S(1)}, u32[]{:S(2)}, u32[]{:S(2)}) collective-permute-start(bf16[272,512]{1,0:T(8,128)(2,1)S(1)} %get-tuple-element.38.refs_0_), channel_id=1, source_target_pairs={{0,8},{1,9},{2,10},{3,11},{4,12},{5,13},{6,14},{7,15},{8,0},{9,1},... | collective-permute-start | bytes 835592 | tf_op jit(solution)/shard_map/ppermute | solution.py:414
  1.5 23.9 %collective-permute-start.11 = (bf16[272,512]{1,0:T(8,128)(2,1)S(1)}, bf16[272,512]{1,0:T(8,128)(2,1)S(1)}, u32[]{:S(2)}, u32[]{:S(2)}) collective-permute-start(bf16[272,512]{1,0:T(8,128)(2,1)S(1)} %get-tuple-element.36.t0_ref.refs_6_.refs_4_.t_ref), channel_id=1, source_target_pairs={{0,8},{1,9},{2,10},{3,11},{4,12},{5,13},{6,14},{7,15},{8,0},{9,1},... | collective-permute-start | bytes 835592 | tf_op jit(solution)/shard_map/ppermute | solution.py:414
  4.1 22.8 %collective-permute-start.6 = (bf16[272,512]{1,0:T(8,128)(2,1)S(1)}, bf16[272,512]{1,0:T(8,128)(2,1)S(1)}, u32[]{:S(2)}, u32[]{:S(2)}) collective-permute-start(bf16[272,512]{1,0:T(8,128)(2,1)S(1)} %get-tuple-element.38.refs_0_), channel_id=1, source_target_pairs={{0,4},{1,5},{2,6},{3,7},{4,0},{5,1},{6,2},{7,3},{8,12},{9,13},{10,... | collective-permute-start | bytes 835592 | tf_op jit(solution)/shard_map/ppermute | solution.py:414
  5.7 19.7 %collective-permute-start.8 = (bf16[256,512]{1,0:T(8,128)(2,1)}, bf16[256,512]{1,0:T(8,128)(2,1)S(1)}, u32[]{:S(2)}, u32[]{:S(2)}) collective-permute-start(bf16[256,512]{1,0:T(8,128)(2,1)} %refs_3_.1), channel_id=1, source_target_pairs={{0,16},{16,0},{1,17},{17,1},{2,18},{18,2},{3,19},{19,3},{4,20},{20... | collective-permute-start | bytes 786440 | tf_op jit(solution)/shard_map/ppermute | solution.py:418
  6.2 21.2 %collective-permute-start = (bf16[272,512]{1,0:T(8,128)(2,1)S(1)}, bf16[272,512]{1,0:T(8,128)(2,1)S(1)}, u32[]{:S(2)}, u32[]{:S(2)}) collective-permute-start(bf16[272,512]{1,0:T(8,128)(2,1)S(1)} %get-tuple-element.36.t0_ref.refs_6_.refs_4_.t_ref), channel_id=1, source_target_pairs={{0,1},{1,0},{2,3},{3,2},{4,5},{5,4},{6,7},{7,6},{8,9},{9,8},{10,11... | collective-permute-start | bytes 835592 | tf_op jit(solution)/shard_map/ppermute | solution.py:414
  20.5 12.9 %collective-permute-start.3 = (bf16[272,512]{1,0:T(8,128)(2,1)S(1)}, bf16[272,512]{1,0:T(8,128)(2,1)S(1)}, u32[]{:S(2)}, u32[]{:S(2)}) collective-permute-start(bf16[272,512]{1,0:T(8,128)(2,1)S(1)} %collective-permute-done.1.refs_0_), channel_id=1, source_target_pairs={{0,4},{1,5},{2,6},{3,7},{4,0},{5,1},{6,2},{7,3},{8,12},{9,13},{10,... | collective-permute-start | bytes 835592 | tf_op jit(solution)/shard_map/ppermute | solution.py:414
  25.4 9.5 %collective-permute-start.12 = (bf16[272,512]{1,0:T(8,128)(2,1)S(1)}, bf16[272,512]{1,0:T(8,128)(2,1)S(1)}, u32[]{:S(2)}, u32[]{:S(2)}) collective-permute-start(bf16[272,512]{1,0:T(8,128)(2,1)S(1)} %collective-permute-done.11.t0_ref), channel_id=1, source_target_pairs={{0,1},{1,0},{2,3},{3,2},{4,5},{5,4},{6,7},{7,6},{8,9},{9,8},{10,11... | collective-permute-start | bytes 835592 | tf_op jit(solution)/shard_map/ppermute | solution.py:414
  25.4 13.3 %collective-permute-start.5 = (bf16[272,512]{1,0:T(8,128)(2,1)S(1)}, bf16[272,512]{1,0:T(8,128)(2,1)S(1)}, u32[]{:S(2)}, u32[]{:S(2)}) collective-permute-start(bf16[272,512]{1,0:T(8,128)(2,1)S(1)} %get-tuple-element.38.refs_0_), channel_id=1, source_target_pairs={{0,2},{1,3},{2,0},{3,1},{4,6},{5,7},{6,4},{7,5},{8,10},{9,11},{10,... | collective-permute-start | bytes 835592 | tf_op jit(solution)/shard_map/ppermute | solution.py:414
  26.9 15.3 %collective-permute-start.7 = (bf16[272,512]{1,0:T(8,128)(2,1)S(1)}, bf16[272,512]{1,0:T(8,128)(2,1)S(1)}, u32[]{:S(2)}, u32[]{:S(2)}) collective-permute-start(bf16[272,512]{1,0:T(8,128)(2,1)S(1)} %collective-permute-done.6.refs_2_), channel_id=1, source_target_pairs={{0,2},{1,3},{2,0},{3,1},{4,6},{5,7},{6,4},{7,5},{8,10},{9,11},{10,... | collective-permute-start | bytes 835592 | tf_op jit(solution)/shard_map/ppermute | solution.py:414
  27.4 14.8 %collective-permute-start.9 = (bf16[256,512]{1,0:T(8,128)(2,1)S(1)}, bf16[256,512]{1,0:T(8,128)(2,1)S(1)}, u32[]{:S(2)}, u32[]{:S(2)}) collective-permute-start(bf16[256,512]{1,0:T(8,128)(2,1)S(1)} %collective-permute-done.8.refs_4_), channel_id=1, source_target_pairs={{0,1},{1,0},{2,3},{3,2},{4,5},{5,4},{6,7},{7,6},{8,9},{9,8},{10,11... | collective-permute-start | bytes 786440 | tf_op jit(solution)/shard_map/ppermute | solution.py:414
  33.4 16.3 %collective-permute-start.2 = (bf16[272,512]{1,0:T(8,128)(2,1)S(1)}, bf16[272,512]{1,0:T(8,128)(2,1)S(1)}, u32[]{:S(2)}, u32[]{:S(2)}) collective-permute-start(bf16[272,512]{1,0:T(8,128)(2,1)S(1)} %collective-permute-done.1.refs_0_), channel_id=1, source_target_pairs={{0,2},{1,3},{2,0},{3,1},{4,6},{5,7},{6,4},{7,5},{8,10},{9,11},{10,... | collective-permute-start | bytes 835592 | tf_op jit(solution)/shard_map/ppermute | solution.py:414
  34.9 23.6 %collective-permute-start.4 = (bf16[272,512]{1,0:T(8,128)(2,1)S(1)}, bf16[272,512]{1,0:T(8,128)(2,1)S(1)}, u32[]{:S(2)}, u32[]{:S(2)}) collective-permute-start(bf16[272,512]{1,0:T(8,128)(2,1)S(1)} %collective-permute-done.3.refs_2_), channel_id=1, source_target_pairs={{0,2},{1,3},{2,0},{3,1},{4,6},{5,7},{6,4},{7,5},{8,10},{9,11},{10,... | collective-permute-start | bytes 835592 | tf_op jit(solution)/shard_map/ppermute | solution.py:414
  38.8 25.2 %collective-permute-start.13 = (bf16[128,512]{1,0:T(8,128)(2,1)S(1)}, bf16[128,512]{1,0:T(8,128)(2,1)S(1)}, u32[]{:S(2)}, u32[]{:S(2)}) collective-permute-start(bf16[128,512]{1,0:T(8,128)(2,1)S(1)} %get-tuple-element.46), channel_id=1, source_target_pairs={{0,6},{1,7},{2,4},{3,5},{4,2},{5,3},{6,0},{7,1},{8,14},{9,15},{10,... | collective-permute-start | bytes 393224 | tf_op jit(solution)/shard_map/ppermute | solution.py:414
  42.3 23.3 %collective-permute-start.14 = (bf16[128,512]{1,0:T(8,128)(2,1)S(1)}, bf16[128,512]{1,0:T(8,128)(2,1)S(1)}, u32[]{:S(2)}, u32[]{:S(2)}) collective-permute-start(bf16[128,512]{1,0:T(8,128)(2,1)S(1)} %get-tuple-element.47), channel_id=1, source_target_pairs={{0,4},{1,5},{2,6},{3,7},{4,0},{5,1},{6,2},{7,3},{8,12},{9,13},{10,... | collective-permute-start | bytes 393224 | tf_op jit(solution)/shard_map/ppermute | solution.py:414
  42.3 23.3 %collective-permute-start.15 = (bf16[128,512]{1,0:T(8,128)(2,1)S(1)}, bf16[128,512]{1,0:T(8,128)(2,1)S(1)}, u32[]{:S(2)}, u32[]{:S(2)}) collective-permute-start(bf16[128,512]{1,0:T(8,128)(2,1)S(1)} %get-tuple-element.48), channel_id=1, source_target_pairs={{0,2},{1,3},{2,0},{3,1},{4,6},{5,7},{6,4},{7,5},{8,10},{9,11},{10,... | collective-permute-start | bytes 393224 | tf_op jit(solution)/shard_map/ppermute | solution.py:414
  49.7 21.1 %collective-permute-start.20 = (bf16[128,512]{1,0:T(8,128)(2,1)S(1)}, bf16[128,512]{1,0:T(8,128)(2,1)S(1)}, u32[]{:S(2)}, u32[]{:S(2)}) collective-permute-start(bf16[128,512]{1,0:T(8,128)(2,1)S(1)} %get-tuple-element.54), channel_id=1, source_target_pairs={{0,6},{1,7},{2,4},{3,5},{4,2},{5,3},{6,0},{7,1},{8,14},{9,15},{10,... | collective-permute-start | bytes 393224 | tf_op jit(solution)/shard_map/ppermute | solution.py:414
  58.5 13.2 %collective-permute-start.21 = (bf16[128,512]{1,0:T(8,128)(2,1)S(1)}, bf16[128,512]{1,0:T(8,128)(2,1)S(1)}, u32[]{:S(2)}, u32[]{:S(2)}) collective-permute-start(bf16[128,512]{1,0:T(8,128)(2,1)S(1)} %get-tuple-element.55), channel_id=1, source_target_pairs={{0,4},{1,5},{2,6},{3,7},{4,0},{5,1},{6,2},{7,3},{8,12},{9,13},{10,... | collective-permute-start | bytes 393224 | tf_op jit(solution)/shard_map/ppermute | solution.py:414
  64.0 9.9 %collective-permute-start.22 = (bf16[128,512]{1,0:T(8,128)(2,1)S(1)}, bf16[128,512]{1,0:T(8,128)(2,1)S(1)}, u32[]{:S(2)}, u32[]{:S(2)}) collective-permute-start(bf16[128,512]{1,0:T(8,128)(2,1)S(1)} %get-tuple-element.56), channel_id=1, source_target_pairs={{0,2},{1,3},{2,0},{3,1},{4,6},{5,7},{6,4},{7,5},{8,10},{9,11},{10,... | collective-permute-start | bytes 393224 | tf_op jit(solution)/shard_map/ppermute | solution.py:414
  65.6 15.5 %collective-permute-start.10 = (bf16[384,512]{1,0:T(8,128)(2,1)S(1)}, bf16[384,512]{1,0:T(8,128)(2,1)S(1)}, u32[]{:S(2)}, u32[]{:S(2)}) collective-permute-start(bf16[384,512]{1,0:T(8,128)(2,1)S(1)} %get-tuple-element.41.g0_ref), channel_id=1, source_target_pairs={{0,1},{1,0},{2,3},{3,2},{4,5},{5,4},{6,7},{7,6},{8,9},{9,8},{10,11... | collective-permute-start | bytes 1179656 | tf_op jit(solution)/shard_map/ppermute | solution.py:414
  73.9 29.5 %collective-permute-start.27 = (bf16[256,512]{1,0:T(8,128)(2,1)S(1)}, bf16[256,512]{1,0:T(8,128)(2,1)S(1)}, u32[]{:S(2)}, u32[]{:S(2)}) collective-permute-start(bf16[256,512]{1,0:T(8,128)(2,1)S(1)} %get-tuple-element.64), channel_id=1, source_target_pairs={{0,1},{1,0},{2,3},{3,2},{4,5},{5,4},{6,7},{7,6},{8,9},{9,8},{10,11... | collective-permute-start | bytes 786440 | tf_op jit(solution)/shard_map/ppermute | solution.py:414
  76.7 15.1 %collective-permute-start.19 = (bf16[128,512]{1,0:T(8,128)(2,1)S(1)}, bf16[128,512]{1,0:T(8,128)(2,1)S(1)}, u32[]{:S(2)}, u32[]{:S(2)}) collective-permute-start(bf16[128,512]{1,0:T(8,128)(2,1)S(1)} %get-tuple-element.53), channel_id=1, source_target_pairs={{0,8},{1,9},{2,10},{3,11},{4,12},{5,13},{6,14},{7,15},{8,0},{9,1},... | collective-permute-start | bytes 393224 | tf_op jit(solution)/shard_map/ppermute | solution.py:414
  77.2 17.4 %collective-permute-start.23 = (bf16[128,512]{1,0:T(8,128)(2,1)S(1)}, bf16[128,512]{1,0:T(8,128)(2,1)S(1)}, u32[]{:S(2)}, u32[]{:S(2)}) collective-permute-start(bf16[128,512]{1,0:T(8,128)(2,1)S(1)} %get-tuple-element.57), channel_id=1, source_target_pairs={{0,10},{1,11},{2,8},{3,9},{4,14},{5,15},{6,12},{7,13},{8,2},{9,3},... | collective-permute-start | bytes 393224 | tf_op jit(solution)/shard_map/ppermute | solution.py:414
  81.0 18.5 %collective-permute-start.24 = (bf16[128,512]{1,0:T(8,128)(2,1)S(1)}, bf16[128,512]{1,0:T(8,128)(2,1)S(1)}, u32[]{:S(2)}, u32[]{:S(2)}) collective-permute-start(bf16[128,512]{1,0:T(8,128)(2,1)S(1)} %get-tuple-element.58), channel_id=1, source_target_pairs={{0,12},{1,13},{2,14},{3,15},{4,8},{5,9},{6,10},{7,11},{8,4},{9,5},... | collective-permute-start | bytes 393224 | tf_op jit(solution)/shard_map/ppermute | solution.py:414
  81.0 21.5 %collective-permute-start.25 = (bf16[128,512]{1,0:T(8,128)(2,1)S(1)}, bf16[128,512]{1,0:T(8,128)(2,1)S(1)}, u32[]{:S(2)}, u32[]{:S(2)}) collective-permute-start(bf16[128,512]{1,0:T(8,128)(2,1)S(1)} %get-tuple-element.59), channel_id=1, source_target_pairs={{0,14},{1,15},{2,12},{3,13},{4,10},{5,11},{6,8},{7,9},{8,6},{9,7},... | collective-permute-start | bytes 393224 | tf_op jit(solution)/shard_map/ppermute | solution.py:414
  (6 other events, 49.8 us)

commit v2 on v1

--- a/solution.py
+++ b/solution.py
@@ -11,6 +11,7 @@
 BF, F32, I32 = jnp.bfloat16, jnp.float32, jnp.int32
 GRANT = 24 << 20
 PAD = 16
+NAMES = 8
 
 
 def whole(shape):
@@ -61,9 +62,9 @@
         copy.start()
     for copy in copies[:3]:
         copy.wait()
-    blank = jnp.zeros((PAD - routes.shape[0], count), F32)
+    blank = jnp.zeros((NAMES - routes.shape[0], count), F32)
     named = jnp.concatenate([routes[...].astype(F32), blank], axis=0).astype(BF)
-    sent_ref[count:] = jnp.concatenate([named, jnp.zeros((PAD, width - count), BF)], axis=1)
+    sent_ref[count:] = jnp.concatenate([named, jnp.zeros((NAMES, width - count), BF)], axis=1)
     rows = [gates[:, s * width : (s + 1) * width] for s in range(tasks)]
     rows.append(jnp.zeros((packed_ref.shape[0] - 2 * units - tasks, width), BF))
     packed_ref[2 * units :] = jnp.concatenate(rows, axis=0)
@@ -86,7 +87,7 @@
         functools.partial(pack_kernel, tasks),
         [
             jax.ShapeDtypeStruct((rows, width), BF),
-            jax.ShapeDtypeStruct((count + PAD, width), BF),
+            jax.ShapeDtypeStruct((count + NAMES, width), BF),
             jax.ShapeDtypeStruct((capacity.shape[0], count), F32),
         ],
         in_specs=[smem, smem] + [pl.BlockSpec(memory_space=pltpu.HBM)] * 6,
@@ -109,7 +110,6 @@
     )
     upper = jnp.where(earlier, 1.0, 0.0).astype(BF)
     slot = lax.broadcasted_iota(I32, (depth, count), 0).astype(F32)
-    codes, keeps = [], []
     for side, sent in enumerate((t0_ref, t1_ref)):
         rel = routes_of(sent, count) ^ me
         named = [rel[k : k + 1] == ids for k in range(2)]
@@ -127,17 +127,18 @@
         picked = jnp.dot(table, sent[0:count], preferred_element_type=F32).astype(BF)
         for m in range(targets):
             outs[m][side * depth : (side + 1) * depth] = picked[m * depth : (m + 1) * depth]
-        for k, here in enumerate(named):
-            rank = jnp.sum(jnp.where(here, ranked, 0.0), axis=0, keepdims=True)
-            keep = rank >= 0.0
-            mine = jnp.logical_and(keep, (rel[k : k + 1] & 1) == 0)
-            place = ((rel[k : k + 1] >> 1) * depth).astype(F32) + rank
-            codes.append(jnp.where(mine, place, -1.0))
-            if side == 0:
+        if side == 0 and len(outs) > targets:
+            keeps, codes = [], []
+            for k, here in enumerate(named):
+                rank = jnp.sum(jnp.where(here, ranked, 0.0), axis=0, keepdims=True)
+                keep = rank >= 0.0
+                place = ((rel[k : k + 1] >> 1) * depth).astype(F32) + rank
+                even = (rel[k : k + 1] & 1) == 0
                 keeps.append(jnp.where(keep, 1.0, 0.0))
-    if len(outs) > targets:
-        blank = jnp.zeros((8 - len(codes) - len(keeps), count), F32)
-        outs[targets][...] = jnp.concatenate(codes + keeps + [blank], axis=0)
+                for parity in (even, jnp.logical_not(even)):
+                    codes.append(jnp.where(jnp.logical_and(keep, parity), place, -1.0))
+            blank = jnp.zeros((8 - len(codes) - len(keeps), count), F32)
+            outs[targets][...] = jnp.concatenate(codes + keeps + [blank], axis=0)
 
 
 def routes_of(sent, count):
@@ -337,65 +338,125 @@
     )(me, pick, rows, sent, g0, g1, shared_gate)
 
 
-def collect_kernel(chips, first, w_ref, *refs):
-    ins, mine_ref, other_ref = refs[:chips], refs[-2], refs[-1]
-    depth = ins[0].shape[0] // 2
+def stack_kernel(*refs):
+    depth = refs[0].shape[0] // 2
+    for i, r in enumerate(refs[:-1]):
+        refs[-1][i * depth : (i + 1) * depth] = r[depth:]
+
+
+def stack(blocks):
+    vmem = pl.BlockSpec(memory_space=pltpu.VMEM)
+    rows, width = blocks[0].shape
+    return call(
+        stack_kernel,
+        jax.ShapeDtypeStruct((len(blocks) * rows // 2, width), BF),
+        in_specs=[vmem] * len(blocks),
+        out_specs=vmem,
+    )(*blocks)
+
+
+def slots_of(masks, depth):
+    lane = lax.broadcasted_iota(I32, (8, len(masks) * depth), 1)
+    ids, before = lane, 0
+    for i, m in enumerate(masks):
+        step = m * depth - i * depth
+        ids = ids + jnp.where(lane >= i * depth, step - before, 0)
+        before = step
+    return ids[0:1].astype(F32)
+
+
+def picks(w_ref, column, ids):
+    return jnp.where(w_ref[:, column : column + 1] == ids, 1.0, 0.0).astype(BF)
+
+
+def collect_kernel(masks, early, first, w_ref, *refs):
+    own, theirs, out = refs[: len(masks)], refs[-2], refs[-1]
+    depth = own[0].shape[0] // 2
     count = w_ref.shape[0]
-    ids = lax.broadcasted_iota(I32, (count, chips * depth), 1).astype(F32)
-    for side, out in ((0, mine_ref), (1, other_ref)):
-        rows = jnp.concatenate([r[side * depth : (side + 1) * depth] for r in ins], axis=0)
-        for k in range(2):
-            column = first + 2 * side + k
-            table = jnp.where(w_ref[:, column : column + 1] == ids, 1.0, 0.0).astype(BF)
-            out[k * count : (k + 1) * count] = jnp.dot(
-                table, rows, preferred_element_type=F32
+    rows = jnp.concatenate([r[0:depth] for r in own] + [theirs[...]], axis=0)
+    own_ids, their_ids = slots_of(masks, depth), slots_of(early, depth)
+    for k in range(2):
+        column = first + 2 * k
+        table = jnp.concatenate(
+            [picks(w_ref, column, own_ids), picks(w_ref, column + 1, their_ids)], axis=1
+        )
+        out[k * count : (k + 1) * count] = jnp.dot(
+            table, rows, preferred_element_type=F32
+        ).astype(BF)
+
+
+def collect(w, masks, blocks, early, theirs, first):
+    vmem = pl.BlockSpec(memory_space=pltpu.VMEM)
+    count, width = w.shape[0], blocks[0].shape[1]
+    slots = theirs.shape[0] + sum(b.shape[0] for b in blocks) // 2
+    return call(
+        functools.partial(collect_kernel, masks, early, first),
+        jax.ShapeDtypeStruct((2 * count, width), BF),
+        in_specs=[vmem] * (2 + len(blocks)),
+        out_specs=vmem,
+        cost_estimate=cost(4 * count * slots * width, 2 * slots * width + 4 * count * width),
+    )(w, *blocks, theirs)
+
+
+def mix_kernel(tasks, gates, late, depth, block, part, w_ref, a_ref, l_ref, s0, s1, x_ref, out_ref, held, sems):
+    first = 4 * gates
+    count = w_ref.shape[0]
+    ids = slots_of(late, depth)
+    row = lax.broadcasted_iota(I32, (part, 4 * part), 0)
+    lane = lax.broadcasted_iota(I32, (part, 4 * part), 1)
+    here = [lane == row + j * part for j in range(4)]
+    copies = []
+    for low in range(0, count, block):
+        span = slice(low, low + block)
+        found = [
+            a_ref[k * count + low : k * count + low + block]
+            + jnp.dot(
+                picks(w_ref.at[span], first + 2 * k + 1, ids),
+                l_ref[...],
+                preferred_element_type=F32,
             ).astype(BF)
-
-
-def collect(w, blocks, first):
-    vmem = pl.BlockSpec(memory_space=pltpu.VMEM)
-    count, width = w.shape[0], blocks[0].shape[1]
-    slots = sum(b.shape[0] for b in blocks)
-    return call(
-        functools.partial(collect_kernel, len(blocks), first),
-        [jax.ShapeDtypeStruct((2 * count, width), BF)] * 2,
-        in_specs=[vmem] * (1 + len(blocks)),
-        out_specs=[vmem] * 2,
-        cost_estimate=cost(4 * count * slots * width, 2 * slots * width + 8 * count * width),
-    )(w, *blocks)
-
-
-def mix_kernel(tasks, gates, w_ref, a0, a1, b0, b1, s0, s1, x_ref, out_ref):
-    rows = [
-        (a0[...] + b0[...]).astype(F32),
-        (a1[...] + b1[...]).astype(F32),
-        s0[...].astype(F32) + s1[...].astype(F32),
-        x_ref[...].astype(F32),
-    ]
-    for s in range(tasks):
-        mixed = None
-        for j, row in enumerate(rows):
-            column = j * gates + s
-            term = w_ref[:, column : column + 1] * row
-            mixed = term if mixed is None else mixed + term
-        out_ref[s] = mixed.astype(BF)
-
-
-def mix(w, mine, theirs, keep, back, far, tasks, block=64):
-    count, full = w.shape
+            for k in range(2)
+        ]
+        found += [(s0[span].astype(F32) + s1[span].astype(F32)).astype(BF), x_ref[span]]
+        for start in range(0, block, part):
+            rows = jnp.concatenate([f[start : start + part] for f in found], axis=0)
+            here_rows = slice(low + start, low + start + part)
+            table = []
+            for s in range(tasks):
+                entry = jnp.zeros((part, 4 * part), F32)
+                for j in range(4):
+                    column = w_ref[here_rows, j * gates + s : j * gates + s + 1]
+                    entry = jnp.where(here[j], column, entry)
+                table.append(entry.astype(BF))
+            mixed = jnp.dot(jnp.concatenate(table, axis=0), rows, preferred_element_type=F32)
+            for s in range(tasks):
+                held[s, here_rows] = mixed[s * part : (s + 1) * part].astype(BF)
+            copies.append(
+                pltpu.make_async_copy(
+                    held.at[:, here_rows], out_ref.at[:, here_rows], sems.at[len(copies)]
+                )
+            )
+            copies[-1].start()
+    for copy in copies:
+        copy.wait()
+
+
+def mix(w, found, late, theirs, keep, back, far, tasks, depth, block=128, part=32):
+    count = w.shape[0]
     width = far.shape[1]
     gates = -(-tasks // PAD) * PAD
-    steps = count // block
-    low = pl.BlockSpec((block, width), lambda i: (i, 0))
-    high = pl.BlockSpec((block, width), lambda i: (i + steps, 0))
-    return call(
-        functools.partial(mix_kernel, tasks, gates),
+    vmem = pl.BlockSpec(memory_space=pltpu.VMEM)
+    return call(
+        functools.partial(mix_kernel, tasks, gates, late, depth, block, part),
         jax.ShapeDtypeStruct((tasks, count, width), BF),
-        grid=(steps,),
-        in_specs=[pl.BlockSpec((block, full), lambda i: (i, 0)), low, high, low, high, low, low, low],
-        out_specs=pl.BlockSpec((tasks, block, width), lambda i: (0, i, 0)),
+        in_specs=[vmem] * 6,
+        out_specs=pl.BlockSpec(memory_space=pltpu.HBM),
+        scratch_shapes=[
+            pltpu.VMEM((tasks, count, width), BF),
+            pltpu.SemaphoreType.DMA((count // part,)),
+        ],
         cost_estimate=cost(8 * tasks * count * width, 2 * (tasks + 8) * count * width),
-    )(w, mine, mine, theirs, theirs, keep, back, far)
+    )(w, found, theirs, keep, back, far)
 
 
 def on_device(
@@ -460,10 +521,26 @@
     far_rows = across(crossing)
     order = tuple(2 * q for q in range(chips))
     w = weights(me, pick, rows, sent, send, summed, shared_gate, tasks, order)
-    mine, other = collect(w, [back[m] for m in range(chips)], 4 * (-(-tasks // PAD) * PAD))
-    theirs = swap(other, 1)
-    mixed = mix(w, mine, theirs, keep, summed, far_rows, tasks)
+    first, last = halves(chips)
+    theirs_first = swap(stack([back[m] for m in first]), 1)
+    theirs_last = swap(stack([back[m] for m in last]), 1)
+    masks = list(range(chips))
+    found = collect(
+        w, masks, [back[m] for m in masks], first, theirs_first, 4 * (-(-tasks // PAD) * PAD)
+    )
+    mixed = mix(w, found, last, theirs_last, keep, summed, far_rows, tasks, depth)
     return mixed.transpose(1, 0, 2)
+
+
+def halves(chips):
+    order = [0] + return_order(chips)
+    return order[: chips // 2], order[chips // 2 :]
+
+
+def return_order(chips):
+    half, near = chips // 2, near_masks(chips)
+    ordered = [m for m in near if m % 2 == 0] + [m for m in near if m % 2]
+    return [half, 1] + [half + m for m in ordered] + [m for m in ordered if m != 1]
 
 
 def near_masks(chips):

time: 116 us -> 108 us (0.931)
  the two profiles are of different devices: /device:TPU:18 before, /device:TPU:0 now
where the time goes in v2:
time: 108 us
  waiting for transfers between devices  57.5 us (53%)
  starting transfers between devices  32.3 us (30%)
  Pallas kernels  18 us (17%)
    ppermute x28, waiting for transfers between devices, swap(): return lax.ppermute(x, 'ep', [(i, i ^ mask) for i in range(experts)])  51.8 us
    ppermute x28, starting transfers between devices, swap(): return lax.ppermute(x, 'ep', [(i, i ^ mask) for i in range(experts)])  29 us
    pallas_call x2, Pallas kernels, expert(): call(functools.partial(expert_kernel, len(xs)), [jax.ShapeDtypeStruct((ro...  6.55 us
    ppermute x2, waiting for transfers between devices, across(): return lax.ppermute(x, 'dp', [(i, groups - 1 - i) for i in range(groups)])  5.62 us
    pallas_call x3, Pallas kernels, shared(): call(functools.partial(shared_kernel, len(shards), units, group, start, g...  3.3 us
    ppermute x2, starting transfers between devices, across(): return lax.ppermute(x, 'dp', [(i, groups - 1 - i) for i in range(groups)])  3.3 us
    pallas_call x1, Pallas kernels, mix(): call(functools.partial(mix_kernel, tasks, gates, late, depth, block, part...  2.5 us
    pallas_call x1, Pallas kernels, load(): call(load_kernel, [jax.ShapeDtypeStruct(a.shape, a.dtype), jax.ShapeDtype...  2.21 us
  transfers between devices with their start and end apart: 30, of which 11 were waited for; matrix products, arithmetic and copies ran while one was open for 0% of the time, Pallas kernels for 13%

profile of v2, /device:TPU:0, one launch (start us, length us, event | category | flops | bytes accessed | tf_op | source)
XLA Modules:
  0.0 108.0 jit_solution(9535076470950867148)
XLA Ops:
  1.1 4.1 %collective-permute-start.11 = (bf16[264,512]{1,0:T(8,128)(2,1)S(1)}, bf16[264,512]{1,0:T(8,128)(2,1)S(1)}, u32[]{:S(2)}, u32[]{:S(2)}) collective-permute-start(bf16[264,512]{1,0:T(8,128)(2,1)S(1)} %get-tuple-element.34.t0_ref.refs_6_.refs_4_.t_ref), channel_id=1, source_target_pairs={{0,8},{1,9},{2,10},{3,11},{4,12},{5,13},{6,14},{7,15},{8,0},{9,1},... | collective-permute-start | bytes 811016 | tf_op jit(solution)/shard_map/ppermute | solution.py:475
  5.4 19.0 %collective-permute-done.11.t0_ref = bf16[264,512]{1,0:T(8,128)(2,1)S(1)} collective-permute-done((bf16[264,512]{1,0:T(8,128)(2,1)S(1)}, bf16[264,512]{1,0:T(8,128)(2,1)S(1)}, u32[]{:S(2)}, u32[]{:S(2)}) %collective-permute-start.11) | collective-permute-done | bytes 270368 | tf_op jit(solution)/shard_map/ppermute | solution.py:475
  24.4 1.8 %collective-permute-start.8 = (bf16[256,512]{1,0:T(8,128)(2,1)}, bf16[256,512]{1,0:T(8,128)(2,1)S(1)}, u32[]{:S(2)}, u32[]{:S(2)}) collective-permute-start(bf16[256,512]{1,0:T(8,128)(2,1)} %refs_3_.1), channel_id=1, source_target_pairs={{0,16},{16,0},{1,17},{17,1},{2,18},{18,2},{3,19},{19,3},{4,20},{20... | collective-permute-start | bytes 786440 | tf_op jit(solution)/shard_map/ppermute | solution.py:479
  26.2 3.4 %collective-permute-done.1.refs_0_ = bf16[272,512]{1,0:T(8,128)(2,1)S(1)} collective-permute-done((bf16[272,512]{1,0:T(8,128)(2,1)S(1)}, bf16[272,512]{1,0:T(8,128)(2,1)S(1)}, u32[]{:S(2)}, u32[]{:S(2)}) %collective-permute-start.1) | collective-permute-done | bytes 278560 | tf_op jit(solution)/shard_map/ppermute | solution.py:475
  30.8 2.4 %collective-permute-start.13 = (bf16[128,512]{1,0:T(8,128)(2,1)S(1)}, bf16[128,512]{1,0:T(8,128)(2,1)S(1)}, u32[]{:S(2)}, u32[]{:S(2)}) collective-permute-start(bf16[128,512]{1,0:T(8,128)(2,1)S(1)} %get-tuple-element.44), channel_id=1, source_target_pairs={{0,6},{1,7},{2,4},{3,5},{4,2},{5,3},{6,0},{7,1},{8,14},{9,15},{10,... | collective-permute-start | bytes 393224 | tf_op jit(solution)/shard_map/ppermute | solution.py:475
  35.5 1.9 %collective-permute-start.20 = (bf16[128,512]{1,0:T(8,128)(2,1)S(1)}, bf16[128,512]{1,0:T(8,128)(2,1)S(1)}, u32[]{:S(2)}, u32[]{:S(2)}) collective-permute-start(bf16[128,512]{1,0:T(8,128)(2,1)S(1)} %get-tuple-element.52), channel_id=1, source_target_pairs={{0,6},{1,7},{2,4},{3,5},{4,2},{5,3},{6,0},{7,1},{8,14},{9,15},{10,... | collective-permute-start | bytes 393224 | tf_op jit(solution)/shard_map/ppermute | solution.py:475
  37.4 7.9 %collective-permute-done.13.refs_2_ = bf16[128,512]{1,0:T(8,128)(2,1)S(1)} collective-permute-done((bf16[128,512]{1,0:T(8,128)(2,1)S(1)}, bf16[128,512]{1,0:T(8,128)(2,1)S(1)}, u32[]{:S(2)}, u32[]{:S(2)}) %collective-permute-start.13) | collective-permute-done | bytes 131104 | tf_op jit(solution)/shard_map/ppermute | solution.py:475
  45.3 1.8 %collective-permute-done.14.refs_3_ = bf16[128,512]{1,0:T(8,128)(2,1)S(1)} collective-permute-done((bf16[128,512]{1,0:T(8,128)(2,1)S(1)}, bf16[128,512]{1,0:T(8,128)(2,1)S(1)}, u32[]{:S(2)}, u32[]{:S(2)}) %collective-permute-start.14) | collective-permute-done | bytes 131104 | tf_op jit(solution)/shard_map/ppermute | solution.py:475
  47.1 1.6 %collective-permute-start.22 = (bf16[128,512]{1,0:T(8,128)(2,1)S(1)}, bf16[128,512]{1,0:T(8,128)(2,1)S(1)}, u32[]{:S(2)}, u32[]{:S(2)}) collective-permute-start(bf16[128,512]{1,0:T(8,128)(2,1)S(1)} %get-tuple-element.54), channel_id=1, source_target_pairs={{0,2},{1,3},{2,0},{3,1},{4,6},{5,7},{6,4},{7,5},{8,10},{9,11},{10,... | collective-permute-start | bytes 393224 | tf_op jit(solution)/shard_map/ppermute | solution.py:475
  48.6 2.2 %shard_map.96 = (bf16[512,2048]{1,0:T(8,128)(2,1)S(1)}, bf16[2048,512]{1,0:T(8,128)(2,1)S(1)}) custom-call(bf16[512,2048]{1,0:T(8,128)(2,1)} %bitcast.6, bf16[2048,512]{1,0:T(8,128)(2,1)} %bitcast.7), custom_call_target="tpu_custom_call" | custom-call | bytes 8388608 | tf_op jit(solution)/shard_map/pallas_call | solution.py:180
  51.4 1.6 %collective-permute-start.2 = (bf16[272,512]{1,0:T(8,128)(2,1)S(1)}, bf16[272,512]{1,0:T(8,128)(2,1)S(1)}, u32[]{:S(2)}, u32[]{:S(2)}) collective-permute-start(bf16[272,512]{1,0:T(8,128)(2,1)S(1)} %collective-permute-done.1.refs_0_), channel_id=1, source_target_pairs={{0,2},{1,3},{2,0},{3,1},{4,6},{5,7},{6,4},{7,5},{8,10},{9,11},{10,... | collective-permute-start | bytes 835592 | tf_op jit(solution)/shard_map/ppermute | solution.py:475
  55.1 3.7 %shard_map.98 = (bf16[128,512]{1,0:T(8,128)(2,1)S(1)}, bf16[128,512]{1,0:T(8,128)(2,1)S(1)}, bf16[128,512]{1,0:T(8,128)(2,1)S(1)}, bf16[128,512]{1,0:T(8,128)(2,1)S(1)}, bf16[128,512]{1,0:T(8,128)(2,1)S(1)}) custom-call(bf16[512,2048]{1,0:T(8,128)(2,1)S(1)} %get-tuple-element.40.w1_ref, bf16[2048,512]{1,0:T(8,128)(2,1)S(1)} %get-tuple-element.41.w2_ref, ...), custom_call_target="tpu_custom_call" | custom-call | flops 2684354560 | bytes 5505024 | tf_op jit(solution)/shard_map/pallas_call | solution.py:223
  58.8 2.8 %shard_map.99 = (bf16[128,512]{1,0:T(8,128)(2,1)S(1)}, bf16[128,512]{1,0:T(8,128)(2,1)S(1)}, bf16[128,512]{1,0:T(8,128)(2,1)S(1)}) custom-call(bf16[512,2048]{1,0:T(8,128)(2,1)S(1)} %get-tuple-element.40.w1_ref, bf16[2048,512]{1,0:T(8,128)(2,1)S(1)} %get-tuple-element.41.w2_ref, bf16[128,512]{1,0:T(8,128)(2,1)S(1)} %collective-permute-done.20.refs_0_, ...), custom_call_target="tpu_custom_call" | custom-call | flops 1610612736 | bytes 4980736 | tf_op jit(solution)/shard_map/pallas_call | solution.py:223
  61.7 1.2 %collective-permute-start.16 = (bf16[128,512]{1,0:T(8,128)(2,1)S(1)}, bf16[128,512]{1,0:T(8,128)(2,1)S(1)}, u32[]{:S(2)}, u32[]{:S(2)}) collective-permute-start(bf16[128,512]{1,0:T(8,128)(2,1)S(1)} %get-tuple-element.48), channel_id=1, source_target_pairs={{0,2},{1,3},{2,0},{3,1},{4,6},{5,7},{6,4},{7,5},{8,10},{9,11},{10,... | collective-permute-start | bytes 393224 | tf_op jit(solution)/shard_map/ppermute | solution.py:475
  62.9 1.6 %collective-permute-start.19 = (bf16[128,512]{1,0:T(8,128)(2,1)S(1)}, bf16[128,512]{1,0:T(8,128)(2,1)S(1)}, u32[]{:S(2)}, u32[]{:S(2)}) collective-permute-start(bf16[128,512]{1,0:T(8,128)(2,1)S(1)} %get-tuple-element.51), channel_id=1, source_target_pairs={{0,8},{1,9},{2,10},{3,11},{4,12},{5,13},{6,14},{7,15},{8,0},{9,1},... | collective-permute-start | bytes 393224 | tf_op jit(solution)/shard_map/ppermute | solution.py:475
  64.5 7.9 %collective-permute-done.7.refs_3_ = bf16[272,512]{1,0:T(8,128)(2,1)S(1)} collective-permute-done((bf16[272,512]{1,0:T(8,128)(2,1)S(1)}, bf16[272,512]{1,0:T(8,128)(2,1)S(1)}, u32[]{:S(2)}, u32[]{:S(2)}) %collective-permute-start.7) | collective-permute-done | bytes 278560 | tf_op jit(solution)/shard_map/ppermute | solution.py:475
  72.4 3.5 %collective-permute-start.24 = (bf16[128,512]{1,0:T(8,128)(2,1)S(1)}, bf16[128,512]{1,0:T(8,128)(2,1)S(1)}, u32[]{:S(2)}, u32[]{:S(2)}) collective-permute-start(bf16[128,512]{1,0:T(8,128)(2,1)S(1)} %get-tuple-element.56), channel_id=1, source_target_pairs={{0,12},{1,13},{2,14},{3,15},{4,8},{5,9},{6,10},{7,11},{8,4},{9,5},... | collective-permute-start | bytes 393224 | tf_op jit(solution)/shard_map/ppermute | solution.py:475
  75.9 1.5 %shard_map.93 = (f32[1024,512]{1,0:T(8,128)S(1)}, bf16[64,512]{1,0:T(8,128)(2,1)S(1)}) custom-call(bf16[272,512]{1,0:T(8,128)(2,1)S(1)} %get-tuple-element.36.refs_0_, bf16[272,512]{1,0:T(8,128)(2,1)S(1)} %collective-permute-done.5.refs_1_, bf16[272,512]{1,0:T(8,128)(2,1)S(1)} %collective-permute-done.6.refs_2_, ...), custom_call_target="tpu_custom_call" | custom-call | flops 1073741824 | bytes 1048576 | tf_op jit(solution)/shard_map/pallas_call | solution.py:276
  81.4 3.9 %collective-permute-start.23 = (bf16[128,512]{1,0:T(8,128)(2,1)S(1)}, bf16[128,512]{1,0:T(8,128)(2,1)S(1)}, u32[]{:S(2)}, u32[]{:S(2)}) collective-permute-start(bf16[128,512]{1,0:T(8,128)(2,1)S(1)} %get-tuple-element.55), channel_id=1, source_target_pairs={{0,10},{1,11},{2,8},{3,9},{4,14},{5,15},{6,12},{7,13},{8,2},{9,3},... | collective-permute-start | bytes 393224 | tf_op jit(solution)/shard_map/ppermute | solution.py:475
  86.0 4.7 %collective-permute-done.18.refs_3_ = bf16[128,512]{1,0:T(8,128)(2,1)S(1)} collective-permute-done((bf16[128,512]{1,0:T(8,128)(2,1)S(1)}, bf16[128,512]{1,0:T(8,128)(2,1)S(1)}, u32[]{:S(2)}, u32[]{:S(2)}) %collective-permute-start.18) | collective-permute-done | bytes 131104 | tf_op jit(solution)/shard_map/ppermute | solution.py:475
  90.8 4.8 %collective-permute-done.25.refs_7_.refs_0_ = bf16[128,512]{1,0:T(8,128)(2,1)S(1)} collective-permute-done((bf16[128,512]{1,0:T(8,128)(2,1)S(1)}, bf16[128,512]{1,0:T(8,128)(2,1)S(1)}, u32[]{:S(2)}, u32[]{:S(2)}) %collective-permute-start.25) | collective-permute-done | bytes 131104 | tf_op jit(solution)/shard_map/ppermute | solution.py:475
  97.2 1.5 %collective-permute-start.29 = (bf16[256,512]{1,0:T(8,128)(2,1)S(1)}, bf16[256,512]{1,0:T(8,128)(2,1)S(1)}, u32[]{:S(2)}, u32[]{:S(2)}) collective-permute-start(bf16[256,512]{1,0:T(8,128)(2,1)S(1)} %add_convert_fusion), channel_id=1, source_target_pairs={{0,16},{16,0},{1,17},{17,1},{2,18},{18,2},{3,19},{19,3},{4,20},{20... | collective-permute-start | bytes 786440 | tf_op jit(solution)/shard_map/ppermute | solution.py:479
  99.9 5.6 %collective-permute-done.29.x_ref = bf16[256,512]{1,0:T(8,128)(2,1)S(1)} collective-permute-done((bf16[256,512]{1,0:T(8,128)(2,1)S(1)}, bf16[256,512]{1,0:T(8,128)(2,1)S(1)}, u32[]{:S(2)}, u32[]{:S(2)}) %collective-permute-start.29) | collective-permute-done | bytes 262176 | tf_op jit(solution)/shard_map/ppermute | solution.py:479
  105.5 2.5 %shard_map.104 = bf16[12,256,512]{2,1,0:T(8,128)(2,1)} custom-call(f32[256,128]{1,0:T(8,128)S(1)} %shard_map.95.w_ref, bf16[512,512]{1,0:T(8,128)(2,1)S(1)} %shard_map.101.a_ref, bf16[256,512]{1,0:T(8,128)(2,1)S(1)} %collective-permute-done.27.l_ref, bf16[256,512]{1,0:T(8,128)(2,1)S(1)} %get-tuple-element.58.s0, ...), custom_call_target="tpu_custom_call" | custom-call | flops 12582912 | bytes 5242880 | tf_op jit(solution)/shard_map/pallas_call | solution.py:449
  (53 shorter events, 14.7 us)
Async XLA Ops:
  1.1 23.2 %collective-permute-start.11 = (bf16[264,512]{1,0:T(8,128)(2,1)S(1)}, bf16[264,512]{1,0:T(8,128)(2,1)S(1)}, u32[]{:S(2)}, u32[]{:S(2)}) collective-permute-start(bf16[264,512]{1,0:T(8,128)(2,1)S(1)} %get-tuple-element.34.t0_ref.refs_6_.refs_4_.t_ref), channel_id=1, source_target_pairs={{0,8},{1,9},{2,10},{3,11},{4,12},{5,13},{6,14},{7,15},{8,0},{9,1},... | collective-permute-start | bytes 811016 | tf_op jit(solution)/shard_map/ppermute | solution.py:475
  5.3 24.3 %collective-permute-start.1 = (bf16[272,512]{1,0:T(8,128)(2,1)S(1)}, bf16[272,512]{1,0:T(8,128)(2,1)S(1)}, u32[]{:S(2)}, u32[]{:S(2)}) collective-permute-start(bf16[272,512]{1,0:T(8,128)(2,1)S(1)} %get-tuple-element.36.refs_0_), channel_id=1, source_target_pairs={{0,8},{1,9},{2,10},{3,11},{4,12},{5,13},{6,14},{7,15},{8,0},{9,1},... | collective-permute-start | bytes 835592 | tf_op jit(solution)/shard_map/ppermute | solution.py:475
  5.3 24.9 %collective-permute-start = (bf16[264,512]{1,0:T(8,128)(2,1)S(1)}, bf16[264,512]{1,0:T(8,128)(2,1)S(1)}, u32[]{:S(2)}, u32[]{:S(2)}) collective-permute-start(bf16[264,512]{1,0:T(8,128)(2,1)S(1)} %get-tuple-element.34.t0_ref.refs_6_.refs_4_.t_ref), channel_id=1, source_target_pairs={{0,1},{1,0},{2,3},{3,2},{4,5},{5,4},{6,7},{7,6},{8,9},{9,8},{10,11... | collective-permute-start | bytes 811016 | tf_op jit(solution)/shard_map/ppermute | solution.py:475
  24.4 8.9 %collective-permute-start.12 = (bf16[264,512]{1,0:T(8,128)(2,1)S(1)}, bf16[264,512]{1,0:T(8,128)(2,1)S(1)}, u32[]{:S(2)}, u32[]{:S(2)}) collective-permute-start(bf16[264,512]{1,0:T(8,128)(2,1)S(1)} %collective-permute-done.11.t0_ref), channel_id=1, source_target_pairs={{0,1},{1,0},{2,3},{3,2},{4,5},{5,4},{6,7},{7,6},{8,9},{9,8},{10,11... | collective-permute-start | bytes 811016 | tf_op jit(solution)/shard_map/ppermute | solution.py:475
  24.4 11.1 %collective-permute-start.6 = (bf16[272,512]{1,0:T(8,128)(2,1)S(1)}, bf16[272,512]{1,0:T(8,128)(2,1)S(1)}, u32[]{:S(2)}, u32[]{:S(2)}) collective-permute-start(bf16[272,512]{1,0:T(8,128)(2,1)S(1)} %get-tuple-element.36.refs_0_), channel_id=1, source_target_pairs={{0,4},{1,5},{2,6},{3,7},{4,0},{5,1},{6,2},{7,3},{8,12},{9,13},{10,... | collective-permute-start | bytes 835592 | tf_op jit(solution)/shard_map/ppermute | solution.py:475
  24.4 10.1 %collective-permute-start.8 = (bf16[256,512]{1,0:T(8,128)(2,1)}, bf16[256,512]{1,0:T(8,128)(2,1)S(1)}, u32[]{:S(2)}, u32[]{:S(2)}) collective-permute-start(bf16[256,512]{1,0:T(8,128)(2,1)} %refs_3_.1), channel_id=1, source_target_pairs={{0,16},{16,0},{1,17},{17,1},{2,18},{18,2},{3,19},{19,3},{4,20},{20... | collective-permute-start | bytes 786440 | tf_op jit(solution)/shard_map/ppermute | solution.py:479
  29.6 21.8 %collective-permute-start.3 = (bf16[272,512]{1,0:T(8,128)(2,1)S(1)}, bf16[272,512]{1,0:T(8,128)(2,1)S(1)}, u32[]{:S(2)}, u32[]{:S(2)}) collective-permute-start(bf16[272,512]{1,0:T(8,128)(2,1)S(1)} %collective-permute-done.1.refs_0_), channel_id=1, source_target_pairs={{0,4},{1,5},{2,6},{3,7},{4,0},{5,1},{6,2},{7,3},{8,12},{9,13},{10,... | collective-permute-start | bytes 835592 | tf_op jit(solution)/shard_map/ppermute | solution.py:475
  30.8 14.5 %collective-permute-start.13 = (bf16[128,512]{1,0:T(8,128)(2,1)S(1)}, bf16[128,512]{1,0:T(8,128)(2,1)S(1)}, u32[]{:S(2)}, u32[]{:S(2)}) collective-permute-start(bf16[128,512]{1,0:T(8,128)(2,1)S(1)} %get-tuple-element.44), channel_id=1, source_target_pairs={{0,6},{1,7},{2,4},{3,5},{4,2},{5,3},{6,0},{7,1},{8,14},{9,15},{10,... | collective-permute-start | bytes 393224 | tf_op jit(solution)/shard_map/ppermute | solution.py:475
  33.2 13.8 %collective-permute-start.14 = (bf16[128,512]{1,0:T(8,128)(2,1)S(1)}, bf16[128,512]{1,0:T(8,128)(2,1)S(1)}, u32[]{:S(2)}, u32[]{:S(2)}) collective-permute-start(bf16[128,512]{1,0:T(8,128)(2,1)S(1)} %get-tuple-element.45), channel_id=1, source_target_pairs={{0,4},{1,5},{2,6},{3,7},{4,0},{5,1},{6,2},{7,3},{8,12},{9,13},{10,... | collective-permute-start | bytes 393224 | tf_op jit(solution)/shard_map/ppermute | solution.py:475
  34.4 16.4 %collective-permute-start.15 = (bf16[128,512]{1,0:T(8,128)(2,1)S(1)}, bf16[128,512]{1,0:T(8,128)(2,1)S(1)}, u32[]{:S(2)}, u32[]{:S(2)}) collective-permute-start(bf16[128,512]{1,0:T(8,128)(2,1)S(1)} %get-tuple-element.46), channel_id=1, source_target_pairs={{0,2},{1,3},{2,0},{3,1},{4,6},{5,7},{6,4},{7,5},{8,10},{9,11},{10,... | collective-permute-start | bytes 393224 | tf_op jit(solution)/shard_map/ppermute | solution.py:475
  35.5 15.9 %collective-permute-start.20 = (bf16[128,512]{1,0:T(8,128)(2,1)S(1)}, bf16[128,512]{1,0:T(8,128)(2,1)S(1)}, u32[]{:S(2)}, u32[]{:S(2)}) collective-permute-start(bf16[128,512]{1,0:T(8,128)(2,1)S(1)} %get-tuple-element.52), channel_id=1, source_target_pairs={{0,6},{1,7},{2,4},{3,5},{4,2},{5,3},{6,0},{7,1},{8,14},{9,15},{10,... | collective-permute-start | bytes 393224 | tf_op jit(solution)/shard_map/ppermute | solution.py:475
  50.9 10.8 %collective-permute-start.5 = (bf16[272,512]{1,0:T(8,128)(2,1)S(1)}, bf16[272,512]{1,0:T(8,128)(2,1)S(1)}, u32[]{:S(2)}, u32[]{:S(2)}) collective-permute-start(bf16[272,512]{1,0:T(8,128)(2,1)S(1)} %get-tuple-element.36.refs_0_), channel_id=1, source_target_pairs={{0,2},{1,3},{2,0},{3,1},{4,6},{5,7},{6,4},{7,5},{8,10},{9,11},{10,... | collective-permute-start | bytes 835592 | tf_op jit(solution)/shard_map/ppermute | solution.py:475
  51.4 11.5 %collective-permute-start.9 = (bf16[256,512]{1,0:T(8,128)(2,1)S(1)}, bf16[256,512]{1,0:T(8,128)(2,1)S(1)}, u32[]{:S(2)}, u32[]{:S(2)}) collective-permute-start(bf16[256,512]{1,0:T(8,128)(2,1)S(1)} %collective-permute-done.8.refs_4_), channel_id=1, source_target_pairs={{0,1},{1,0},{2,3},{3,2},{4,5},{5,4},{6,7},{7,6},{8,9},{9,8},{10,11... | collective-permute-start | bytes 786440 | tf_op jit(solution)/shard_map/ppermute | solution.py:475
  51.4 26.0 %collective-permute-start.2 = (bf16[272,512]{1,0:T(8,128)(2,1)S(1)}, bf16[272,512]{1,0:T(8,128)(2,1)S(1)}, u32[]{:S(2)}, u32[]{:S(2)}) collective-permute-start(bf16[272,512]{1,0:T(8,128)(2,1)S(1)} %collective-permute-done.1.refs_0_), channel_id=1, source_target_pairs={{0,2},{1,3},{2,0},{3,1},{4,6},{5,7},{6,4},{7,5},{8,10},{9,11},{10,... | collective-permute-start | bytes 835592 | tf_op jit(solution)/shard_map/ppermute | solution.py:475
  53.0 19.4 %collective-permute-start.7 = (bf16[272,512]{1,0:T(8,128)(2,1)S(1)}, bf16[272,512]{1,0:T(8,128)(2,1)S(1)}, u32[]{:S(2)}, u32[]{:S(2)}) collective-permute-start(bf16[272,512]{1,0:T(8,128)(2,1)S(1)} %collective-permute-done.6.refs_2_), channel_id=1, source_target_pairs={{0,2},{1,3},{2,0},{3,1},{4,6},{5,7},{6,4},{7,5},{8,10},{9,11},{10,... | collective-permute-start | bytes 835592 | tf_op jit(solution)/shard_map/ppermute | solution.py:475
  54.2 24.2 %collective-permute-start.4 = (bf16[272,512]{1,0:T(8,128)(2,1)S(1)}, bf16[272,512]{1,0:T(8,128)(2,1)S(1)}, u32[]{:S(2)}, u32[]{:S(2)}) collective-permute-start(bf16[272,512]{1,0:T(8,128)(2,1)S(1)} %collective-permute-done.3.refs_2_), channel_id=1, source_target_pairs={{0,2},{1,3},{2,0},{3,1},{4,6},{5,7},{6,4},{7,5},{8,10},{9,11},{10,... | collective-permute-start | bytes 835592 | tf_op jit(solution)/shard_map/ppermute | solution.py:475
  61.7 18.7 %collective-permute-start.16 = (bf16[128,512]{1,0:T(8,128)(2,1)S(1)}, bf16[128,512]{1,0:T(8,128)(2,1)S(1)}, u32[]{:S(2)}, u32[]{:S(2)}) collective-permute-start(bf16[128,512]{1,0:T(8,128)(2,1)S(1)} %get-tuple-element.48), channel_id=1, source_target_pairs={{0,2},{1,3},{2,0},{3,1},{4,6},{5,7},{6,4},{7,5},{8,10},{9,11},{10,... | collective-permute-start | bytes 393224 | tf_op jit(solution)/shard_map/ppermute | solution.py:475
  62.9 18.5 %collective-permute-start.19 = (bf16[128,512]{1,0:T(8,128)(2,1)S(1)}, bf16[128,512]{1,0:T(8,128)(2,1)S(1)}, u32[]{:S(2)}, u32[]{:S(2)}) collective-permute-start(bf16[128,512]{1,0:T(8,128)(2,1)S(1)} %get-tuple-element.51), channel_id=1, source_target_pairs={{0,8},{1,9},{2,10},{3,11},{4,12},{5,13},{6,14},{7,15},{8,0},{9,1},... | collective-permute-start | bytes 393224 | tf_op jit(solution)/shard_map/ppermute | solution.py:475
  72.4 12.9 %collective-permute-start.24 = (bf16[128,512]{1,0:T(8,128)(2,1)S(1)}, bf16[128,512]{1,0:T(8,128)(2,1)S(1)}, u32[]{:S(2)}, u32[]{:S(2)}) collective-permute-start(bf16[128,512]{1,0:T(8,128)(2,1)S(1)} %get-tuple-element.56), channel_id=1, source_target_pairs={{0,12},{1,13},{2,14},{3,15},{4,8},{5,9},{6,10},{7,11},{8,4},{9,5},... | collective-permute-start | bytes 393224 | tf_op jit(solution)/shard_map/ppermute | solution.py:475
  79.3 17.9 %collective-permute-start.28 = (bf16[256,512]{1,0:T(8,128)(2,1)S(1)}, bf16[256,512]{1,0:T(8,128)(2,1)S(1)}, u32[]{:S(2)}, u32[]{:S(2)}) collective-permute-start(bf16[256,512]{1,0:T(8,128)(2,1)S(1)} %get-tuple-element.60), channel_id=1, source_target_pairs={{0,1},{1,0},{2,3},{3,2},{4,5},{5,4},{6,7},{7,6},{8,9},{9,8},{10,11... | collective-permute-start | bytes 786440 | tf_op jit(solution)/shard_map/ppermute | solution.py:475
  80.3 10.4 %collective-permute-start.18 = (bf16[128,512]{1,0:T(8,128)(2,1)S(1)}, bf16[128,512]{1,0:T(8,128)(2,1)S(1)}, u32[]{:S(2)}, u32[]{:S(2)}) collective-permute-start(bf16[128,512]{1,0:T(8,128)(2,1)S(1)} %get-tuple-element.50), channel_id=1, source_target_pairs={{0,6},{1,7},{2,4},{3,5},{4,2},{5,3},{6,0},{7,1},{8,14},{9,15},{10,... | collective-permute-start | bytes 393224 | tf_op jit(solution)/shard_map/ppermute | solution.py:475
  81.4 9.4 %collective-permute-start.23 = (bf16[128,512]{1,0:T(8,128)(2,1)S(1)}, bf16[128,512]{1,0:T(8,128)(2,1)S(1)}, u32[]{:S(2)}, u32[]{:S(2)}) collective-permute-start(bf16[128,512]{1,0:T(8,128)(2,1)S(1)} %get-tuple-element.55), channel_id=1, source_target_pairs={{0,10},{1,11},{2,8},{3,9},{4,14},{5,15},{6,12},{7,13},{8,2},{9,3},... | collective-permute-start | bytes 393224 | tf_op jit(solution)/shard_map/ppermute | solution.py:475
  85.3 10.3 %collective-permute-start.25 = (bf16[128,512]{1,0:T(8,128)(2,1)S(1)}, bf16[128,512]{1,0:T(8,128)(2,1)S(1)}, u32[]{:S(2)}, u32[]{:S(2)}) collective-permute-start(bf16[128,512]{1,0:T(8,128)(2,1)S(1)} %get-tuple-element.57), channel_id=1, source_target_pairs={{0,14},{1,15},{2,12},{3,13},{4,10},{5,11},{6,8},{7,9},{8,6},{9,7},... | collective-permute-start | bytes 393224 | tf_op jit(solution)/shard_map/ppermute | solution.py:475
  86.0 13.3 %collective-permute-start.26 = (bf16[256,512]{1,0:T(8,128)(2,1)S(1)}, bf16[256,512]{1,0:T(8,128)(2,1)S(1)}, u32[]{:S(2)}, u32[]{:S(2)}) collective-permute-start(bf16[256,512]{1,0:T(8,128)(2,1)S(1)} %shard_map.100), channel_id=1, source_target_pairs={{0,1},{1,0},{2,3},{3,2},{4,5},{5,4},{6,7},{7,6},{8,9},{9,8},{10,11... | collective-permute-start | bytes 786440 | tf_op jit(solution)/shard_map/ppermute | solution.py:475
  (7 other events, 39.4 us)

commit v3 on v2

--- a/solution.py
+++ b/solution.py
@@ -398,13 +398,34 @@
     )(w, *blocks, theirs)
 
 
-def mix_kernel(tasks, gates, late, depth, block, part, w_ref, a_ref, l_ref, s0, s1, x_ref, out_ref, held, sems):
+def table_kernel(tasks, gates, part, w_ref, m_ref):
+    row = lax.broadcasted_iota(I32, (part, 4 * part), 0)
+    lane = lax.broadcasted_iota(I32, (part, 4 * part), 1)
+    here = [lane == row + j * part for j in range(4)]
+    for start in range(0, w_ref.shape[0], part):
+        for s in range(tasks):
+            entry = jnp.zeros((part, 4 * part), F32)
+            for j in range(4):
+                column = w_ref[start : start + part, j * gates + s : j * gates + s + 1]
+                entry = jnp.where(here[j], column, entry)
+            place = start * tasks + s * part
+            m_ref[place : place + part] = entry.astype(BF)
+
+
+def table(w, tasks, part=32):
+    vmem = pl.BlockSpec(memory_space=pltpu.VMEM)
+    return call(
+        functools.partial(table_kernel, tasks, -(-tasks // PAD) * PAD, part),
+        jax.ShapeDtypeStruct((w.shape[0] * tasks, 4 * part), BF),
+        in_specs=[vmem],
+        out_specs=vmem,
+    )(w)
+
+
+def mix_kernel(tasks, gates, late, depth, block, part, w_ref, m_ref, a_ref, l_ref, s0, s1, x_ref, out_ref, held, sems):
     first = 4 * gates
     count = w_ref.shape[0]
     ids = slots_of(late, depth)
-    row = lax.broadcasted_iota(I32, (part, 4 * part), 0)
-    lane = lax.broadcasted_iota(I32, (part, 4 * part), 1)
-    here = [lane == row + j * part for j in range(4)]
     copies = []
     for low in range(0, count, block):
         span = slice(low, low + block)
@@ -421,14 +442,9 @@
         for start in range(0, block, part):
             rows = jnp.concatenate([f[start : start + part] for f in found], axis=0)
             here_rows = slice(low + start, low + start + part)
-            table = []
-            for s in range(tasks):
-                entry = jnp.zeros((part, 4 * part), F32)
-                for j in range(4):
-                    column = w_ref[here_rows, j * gates + s : j * gates + s + 1]
-                    entry = jnp.where(here[j], column, entry)
-                table.append(entry.astype(BF))
-            mixed = jnp.dot(jnp.concatenate(table, axis=0), rows, preferred_element_type=F32)
+            size = tasks * part
+            table = m_ref[len(copies) * size : (len(copies) + 1) * size]
+            mixed = jnp.dot(table, rows, preferred_element_type=F32)
             for s in range(tasks):
                 held[s, here_rows] = mixed[s * part : (s + 1) * part].astype(BF)
             copies.append(
@@ -441,7 +457,7 @@
         copy.wait()
 
 
-def mix(w, found, late, theirs, keep, back, far, tasks, depth, block=128, part=32):
+def mix(w, spread, found, late, theirs, keep, back, far, tasks, depth, block=128, part=32):
     count = w.shape[0]
     width = far.shape[1]
     gates = -(-tasks // PAD) * PAD
@@ -449,14 +465,14 @@
     return call(
         functools.partial(mix_kernel, tasks, gates, late, depth, block, part),
         jax.ShapeDtypeStruct((tasks, count, width), BF),
-        in_specs=[vmem] * 6,
+        in_specs=[vmem] * 7,
         out_specs=pl.BlockSpec(memory_space=pltpu.HBM),
         scratch_shapes=[
             pltpu.VMEM((tasks, count, width), BF),
             pltpu.SemaphoreType.DMA((count // part,)),
         ],
         cost_estimate=cost(8 * tasks * count * width, 2 * (tasks + 8) * count * width),
-    )(w, found, theirs, keep, back, far)
+    )(w, spread, found, theirs, keep, back, far)
 
 
 def on_device(
@@ -528,7 +544,7 @@
     found = collect(
         w, masks, [back[m] for m in masks], first, theirs_first, 4 * (-(-tasks // PAD) * PAD)
     )
-    mixed = mix(w, found, last, theirs_last, keep, summed, far_rows, tasks, depth)
+    mixed = mix(w, table(w, tasks), found, last, theirs_last, keep, summed, far_rows, tasks, depth)
     return mixed.transpose(1, 0, 2)
 
 

time: 108 us -> 108 us (level)
  waiting for transfers between devices: 57.5 us -> 56.1 us
  Pallas kernels: 18 us -> 19.1 us
    ppermute x2, waiting for transfers between devices: 5.62 us -> 4.27 us  [across(): return lax.ppermute(x, 'dp', [(i, groups - 1 - i) for i in range(groups)])]
    pallas_call x0 -> x1, Pallas kernels: none -> 1.35 us  [table(): call(functools.partial(table_kernel, tasks, -(-tasks // PAD) * PAD, part)...]
  transfers between devices with their start and end apart: 30 -> 30, of which waited for: 11 -> 11; matrix products, arithmetic and copies ran while one was open for 0% -> 0% of each run, Pallas kernels for 13% -> 15%
where the time goes in v3:
time: 108 us
  waiting for transfers between devices  56.1 us (52%)
  starting transfers between devices  32.3 us (30%)
  Pallas kernels  19.1 us (18%)
    ppermute x28, waiting for transfers between devices, swap(): return lax.ppermute(x, 'ep', [(i, i ^ mask) for i in range(experts)])  51.8 us
    ppermute x28, starting transfers between devices, swap(): return lax.ppermute(x, 'ep', [(i, i ^ mask) for i in range(experts)])  29 us
    pallas_call x2, Pallas kernels, expert(): call(functools.partial(expert_kernel, len(xs)), [jax.ShapeDtypeStruct((ro...  6.57 us
    ppermute x2, waiting for transfers between devices, across(): return lax.ppermute(x, 'dp', [(i, groups - 1 - i) for i in range(groups)])  4.27 us
    pallas_call x3, Pallas kernels, shared(): call(functools.partial(shared_kernel, len(shards), units, group, start, g...  3.3 us
    ppermute x2, starting transfers between devices, across(): return lax.ppermute(x, 'dp', [(i, groups - 1 - i) for i in range(groups)])  3.3 us
    pallas_call x1, Pallas kernels, mix(): call(functools.partial(mix_kernel, tasks, gates, late, depth, block, part...  2.28 us
    pallas_call x1, Pallas kernels, load(): call(load_kernel, [jax.ShapeDtypeStruct(a.shape, a.dtype), jax.ShapeDtype...  2.21 us
  transfers between devices with their start and end apart: 30, of which 11 were waited for; matrix products, arithmetic and copies ran while one was open for 0% of the time, Pallas kernels for 15%

profile of v3, /device:TPU:0, one launch (start us, length us, event | category | flops | bytes accessed | tf_op | source)
XLA Modules:
  0.0 107.8 jit_solution(11505119374114611885)
XLA Ops:
  1.1 4.1 %collective-permute-start.11 = (bf16[264,512]{1,0:T(8,128)(2,1)S(1)}, bf16[264,512]{1,0:T(8,128)(2,1)S(1)}, u32[]{:S(2)}, u32[]{:S(2)}) collective-permute-start(bf16[264,512]{1,0:T(8,128)(2,1)S(1)} %get-tuple-element.34.t0_ref.refs_6_.refs_4_.t_ref), channel_id=1, source_target_pairs={{0,8},{1,9},{2,10},{3,11},{4,12},{5,13},{6,14},{7,15},{8,0},{9,1},... | collective-permute-start | bytes 811016 | tf_op jit(solution)/shard_map/ppermute | solution.py:491
  5.4 19.0 %collective-permute-done.11.t0_ref = bf16[264,512]{1,0:T(8,128)(2,1)S(1)} collective-permute-done((bf16[264,512]{1,0:T(8,128)(2,1)S(1)}, bf16[264,512]{1,0:T(8,128)(2,1)S(1)}, u32[]{:S(2)}, u32[]{:S(2)}) %collective-permute-start.11) | collective-permute-done | bytes 270368 | tf_op jit(solution)/shard_map/ppermute | solution.py:491
  24.4 1.8 %collective-permute-start.8 = (bf16[256,512]{1,0:T(8,128)(2,1)}, bf16[256,512]{1,0:T(8,128)(2,1)S(1)}, u32[]{:S(2)}, u32[]{:S(2)}) collective-permute-start(bf16[256,512]{1,0:T(8,128)(2,1)} %refs_3_.1), channel_id=1, source_target_pairs={{0,16},{16,0},{1,17},{17,1},{2,18},{18,2},{3,19},{19,3},{4,20},{20... | collective-permute-start | bytes 786440 | tf_op jit(solution)/shard_map/ppermute | solution.py:495
  26.2 3.4 %collective-permute-done.1.refs_0_ = bf16[272,512]{1,0:T(8,128)(2,1)S(1)} collective-permute-done((bf16[272,512]{1,0:T(8,128)(2,1)S(1)}, bf16[272,512]{1,0:T(8,128)(2,1)S(1)}, u32[]{:S(2)}, u32[]{:S(2)}) %collective-permute-start.1) | collective-permute-done | bytes 278560 | tf_op jit(solution)/shard_map/ppermute | solution.py:491
  30.8 2.4 %collective-permute-start.13 = (bf16[128,512]{1,0:T(8,128)(2,1)S(1)}, bf16[128,512]{1,0:T(8,128)(2,1)S(1)}, u32[]{:S(2)}, u32[]{:S(2)}) collective-permute-start(bf16[128,512]{1,0:T(8,128)(2,1)S(1)} %get-tuple-element.44), channel_id=1, source_target_pairs={{0,6},{1,7},{2,4},{3,5},{4,2},{5,3},{6,0},{7,1},{8,14},{9,15},{10,... | collective-permute-start | bytes 393224 | tf_op jit(solution)/shard_map/ppermute | solution.py:491
  35.5 1.9 %collective-permute-start.20 = (bf16[128,512]{1,0:T(8,128)(2,1)S(1)}, bf16[128,512]{1,0:T(8,128)(2,1)S(1)}, u32[]{:S(2)}, u32[]{:S(2)}) collective-permute-start(bf16[128,512]{1,0:T(8,128)(2,1)S(1)} %get-tuple-element.52), channel_id=1, source_target_pairs={{0,6},{1,7},{2,4},{3,5},{4,2},{5,3},{6,0},{7,1},{8,14},{9,15},{10,... | collective-permute-start | bytes 393224 | tf_op jit(solution)/shard_map/ppermute | solution.py:491
  37.4 7.9 %collective-permute-done.13.refs_2_ = bf16[128,512]{1,0:T(8,128)(2,1)S(1)} collective-permute-done((bf16[128,512]{1,0:T(8,128)(2,1)S(1)}, bf16[128,512]{1,0:T(8,128)(2,1)S(1)}, u32[]{:S(2)}, u32[]{:S(2)}) %collective-permute-start.13) | collective-permute-done | bytes 131104 | tf_op jit(solution)/shard_map/ppermute | solution.py:491
  45.3 1.8 %collective-permute-done.14.refs_3_ = bf16[128,512]{1,0:T(8,128)(2,1)S(1)} collective-permute-done((bf16[128,512]{1,0:T(8,128)(2,1)S(1)}, bf16[128,512]{1,0:T(8,128)(2,1)S(1)}, u32[]{:S(2)}, u32[]{:S(2)}) %collective-permute-start.14) | collective-permute-done | bytes 131104 | tf_op jit(solution)/shard_map/ppermute | solution.py:491
  47.1 1.6 %collective-permute-start.22 = (bf16[128,512]{1,0:T(8,128)(2,1)S(1)}, bf16[128,512]{1,0:T(8,128)(2,1)S(1)}, u32[]{:S(2)}, u32[]{:S(2)}) collective-permute-start(bf16[128,512]{1,0:T(8,128)(2,1)S(1)} %get-tuple-element.54), channel_id=1, source_target_pairs={{0,2},{1,3},{2,0},{3,1},{4,6},{5,7},{6,4},{7,5},{8,10},{9,11},{10,... | collective-permute-start | bytes 393224 | tf_op jit(solution)/shard_map/ppermute | solution.py:491
  48.6 2.2 %shard_map.97 = (bf16[512,2048]{1,0:T(8,128)(2,1)S(1)}, bf16[2048,512]{1,0:T(8,128)(2,1)S(1)}) custom-call(bf16[512,2048]{1,0:T(8,128)(2,1)} %bitcast.6, bf16[2048,512]{1,0:T(8,128)(2,1)} %bitcast.7), custom_call_target="tpu_custom_call" | custom-call | bytes 8388608 | tf_op jit(solution)/shard_map/pallas_call | solution.py:180
  51.4 1.6 %collective-permute-start.2 = (bf16[272,512]{1,0:T(8,128)(2,1)S(1)}, bf16[272,512]{1,0:T(8,128)(2,1)S(1)}, u32[]{:S(2)}, u32[]{:S(2)}) collective-permute-start(bf16[272,512]{1,0:T(8,128)(2,1)S(1)} %collective-permute-done.1.refs_0_), channel_id=1, source_target_pairs={{0,2},{1,3},{2,0},{3,1},{4,6},{5,7},{6,4},{7,5},{8,10},{9,11},{10,... | collective-permute-start | bytes 835592 | tf_op jit(solution)/shard_map/ppermute | solution.py:491
  55.1 3.7 %shard_map.99 = (bf16[128,512]{1,0:T(8,128)(2,1)S(1)}, bf16[128,512]{1,0:T(8,128)(2,1)S(1)}, bf16[128,512]{1,0:T(8,128)(2,1)S(1)}, bf16[128,512]{1,0:T(8,128)(2,1)S(1)}, bf16[128,512]{1,0:T(8,128)(2,1)S(1)}) custom-call(bf16[512,2048]{1,0:T(8,128)(2,1)S(1)} %get-tuple-element.40.w1_ref, bf16[2048,512]{1,0:T(8,128)(2,1)S(1)} %get-tuple-element.41.w2_ref, ...), custom_call_target="tpu_custom_call" | custom-call | flops 2684354560 | bytes 5505024 | tf_op jit(solution)/shard_map/pallas_call | solution.py:223
  58.8 2.8 %shard_map.100 = (bf16[128,512]{1,0:T(8,128)(2,1)S(1)}, bf16[128,512]{1,0:T(8,128)(2,1)S(1)}, bf16[128,512]{1,0:T(8,128)(2,1)S(1)}) custom-call(bf16[512,2048]{1,0:T(8,128)(2,1)S(1)} %get-tuple-element.40.w1_ref, bf16[2048,512]{1,0:T(8,128)(2,1)S(1)} %get-tuple-element.41.w2_ref, bf16[128,512]{1,0:T(8,128)(2,1)S(1)} %collective-permute-done.20.refs_0_, ...), custom_call_target="tpu_custom_call" | custom-call | flops 1610612736 | bytes 4980736 | tf_op jit(solution)/shard_map/pallas_call | solution.py:223
  62.9 1.6 %collective-permute-start.19 = (bf16[128,512]{1,0:T(8,128)(2,1)S(1)}, bf16[128,512]{1,0:T(8,128)(2,1)S(1)}, u32[]{:S(2)}, u32[]{:S(2)}) collective-permute-start(bf16[128,512]{1,0:T(8,128)(2,1)S(1)} %get-tuple-element.51), channel_id=1, source_target_pairs={{0,8},{1,9},{2,10},{3,11},{4,12},{5,13},{6,14},{7,15},{8,0},{9,1},... | collective-permute-start | bytes 393224 | tf_op jit(solution)/shard_map/ppermute | solution.py:491
  64.5 7.9 %collective-permute-done.7.refs_3_ = bf16[272,512]{1,0:T(8,128)(2,1)S(1)} collective-permute-done((bf16[272,512]{1,0:T(8,128)(2,1)S(1)}, bf16[272,512]{1,0:T(8,128)(2,1)S(1)}, u32[]{:S(2)}, u32[]{:S(2)}) %collective-permute-start.7) | collective-permute-done | bytes 278560 | tf_op jit(solution)/shard_map/ppermute | solution.py:491
  72.4 3.5 %collective-permute-start.24 = (bf16[128,512]{1,0:T(8,128)(2,1)S(1)}, bf16[128,512]{1,0:T(8,128)(2,1)S(1)}, u32[]{:S(2)}, u32[]{:S(2)}) collective-permute-start(bf16[128,512]{1,0:T(8,128)(2,1)S(1)} %get-tuple-element.56), channel_id=1, source_target_pairs={{0,12},{1,13},{2,14},{3,15},{4,8},{5,9},{6,10},{7,11},{8,4},{9,5},... | collective-permute-start | bytes 393224 | tf_op jit(solution)/shard_map/ppermute | solution.py:491
  75.9 1.5 %shard_map.93 = (f32[1024,512]{1,0:T(8,128)S(1)}, bf16[64,512]{1,0:T(8,128)(2,1)S(1)}) custom-call(bf16[272,512]{1,0:T(8,128)(2,1)S(1)} %get-tuple-element.36.refs_0_, bf16[272,512]{1,0:T(8,128)(2,1)S(1)} %collective-permute-done.5.refs_1_, bf16[272,512]{1,0:T(8,128)(2,1)S(1)} %collective-permute-done.6.refs_2_, ...), custom_call_target="tpu_custom_call" | custom-call | flops 1073741824 | bytes 1048576 | tf_op jit(solution)/shard_map/pallas_call | solution.py:276
  81.4 3.9 %collective-permute-start.23 = (bf16[128,512]{1,0:T(8,128)(2,1)S(1)}, bf16[128,512]{1,0:T(8,128)(2,1)S(1)}, u32[]{:S(2)}, u32[]{:S(2)}) collective-permute-start(bf16[128,512]{1,0:T(8,128)(2,1)S(1)} %get-tuple-element.55), channel_id=1, source_target_pairs={{0,10},{1,11},{2,8},{3,9},{4,14},{5,15},{6,12},{7,13},{8,2},{9,3},... | collective-permute-start | bytes 393224 | tf_op jit(solution)/shard_map/ppermute | solution.py:491
  86.0 4.7 %collective-permute-done.18.refs_3_ = bf16[128,512]{1,0:T(8,128)(2,1)S(1)} collective-permute-done((bf16[128,512]{1,0:T(8,128)(2,1)S(1)}, bf16[128,512]{1,0:T(8,128)(2,1)S(1)}, u32[]{:S(2)}, u32[]{:S(2)}) %collective-permute-start.18) | collective-permute-done | bytes 131104 | tf_op jit(solution)/shard_map/ppermute | solution.py:491
  90.8 4.8 %collective-permute-done.25.refs_7_.refs_0_ = bf16[128,512]{1,0:T(8,128)(2,1)S(1)} collective-permute-done((bf16[128,512]{1,0:T(8,128)(2,1)S(1)}, bf16[128,512]{1,0:T(8,128)(2,1)S(1)}, u32[]{:S(2)}, u32[]{:S(2)}) %collective-permute-start.25) | collective-permute-done | bytes 131104 | tf_op jit(solution)/shard_map/ppermute | solution.py:491
  97.2 1.5 %collective-permute-start.29 = (bf16[256,512]{1,0:T(8,128)(2,1)S(1)}, bf16[256,512]{1,0:T(8,128)(2,1)S(1)}, u32[]{:S(2)}, u32[]{:S(2)}) collective-permute-start(bf16[256,512]{1,0:T(8,128)(2,1)S(1)} %add_convert_fusion), channel_id=1, source_target_pairs={{0,16},{16,0},{1,17},{17,1},{2,18},{18,2},{3,19},{19,3},{4,20},{20... | collective-permute-start | bytes 786440 | tf_op jit(solution)/shard_map/ppermute | solution.py:495
  99.3 1.4 %shard_map.96.m_ref = bf16[3072,128]{1,0:T(8,128)(2,1)S(1)} custom-call(f32[256,128]{1,0:T(8,128)S(1)} %shard_map.95.w_ref), custom_call_target="tpu_custom_call" | custom-call | tf_op jit(solution)/shard_map/pallas_call | solution.py:417
  101.3 4.3 %collective-permute-done.29.x_ref = bf16[256,512]{1,0:T(8,128)(2,1)S(1)} collective-permute-done((bf16[256,512]{1,0:T(8,128)(2,1)S(1)}, bf16[256,512]{1,0:T(8,128)(2,1)S(1)}, u32[]{:S(2)}, u32[]{:S(2)}) %collective-permute-start.29) | collective-permute-done | bytes 262176 | tf_op jit(solution)/shard_map/ppermute | solution.py:495
  105.5 2.3 %shard_map.105 = bf16[12,256,512]{2,1,0:T(8,128)(2,1)} custom-call(f32[256,128]{1,0:T(8,128)S(1)} %shard_map.95.w_ref, bf16[3072,128]{1,0:T(8,128)(2,1)S(1)} %shard_map.96.m_ref, bf16[512,512]{1,0:T(8,128)(2,1)S(1)} %shard_map.102.a_ref, bf16[256,512]{1,0:T(8,128)(2,1)S(1)} %collective-permute-done.27.l_ref, bf16[256,512]{1,0:T(8,128)(2,1)S(1)} %get-tuple-element.58.s0, ...), custom_call_target="tpu_custom_call" | custom-call | flops 12582912 | bytes 5242880 | tf_op jit(solution)/shard_map/pallas_call | solution.py:465
  (54 shorter events, 16.0 us)
Async XLA Ops:
  1.1 23.2 %collective-permute-start.11 = (bf16[264,512]{1,0:T(8,128)(2,1)S(1)}, bf16[264,512]{1,0:T(8,128)(2,1)S(1)}, u32[]{:S(2)}, u32[]{:S(2)}) collective-permute-start(bf16[264,512]{1,0:T(8,128)(2,1)S(1)} %get-tuple-element.34.t0_ref.refs_6_.refs_4_.t_ref), channel_id=1, source_target_pairs={{0,8},{1,9},{2,10},{3,11},{4,12},{5,13},{6,14},{7,15},{8,0},{9,1},... | collective-permute-start | bytes 811016 | tf_op jit(solution)/shard_map/ppermute | solution.py:491
  5.3 24.3 %collective-permute-start.1 = (bf16[272,512]{1,0:T(8,128)(2,1)S(1)}, bf16[272,512]{1,0:T(8,128)(2,1)S(1)}, u32[]{:S(2)}, u32[]{:S(2)}) collective-permute-start(bf16[272,512]{1,0:T(8,128)(2,1)S(1)} %get-tuple-element.36.refs_0_), channel_id=1, source_target_pairs={{0,8},{1,9},{2,10},{3,11},{4,12},{5,13},{6,14},{7,15},{8,0},{9,1},... | collective-permute-start | bytes 835592 | tf_op jit(solution)/shard_map/ppermute | solution.py:491
  5.3 24.9 %collective-permute-start = (bf16[264,512]{1,0:T(8,128)(2,1)S(1)}, bf16[264,512]{1,0:T(8,128)(2,1)S(1)}, u32[]{:S(2)}, u32[]{:S(2)}) collective-permute-start(bf16[264,512]{1,0:T(8,128)(2,1)S(1)} %get-tuple-element.34.t0_ref.refs_6_.refs_4_.t_ref), channel_id=1, source_target_pairs={{0,1},{1,0},{2,3},{3,2},{4,5},{5,4},{6,7},{7,6},{8,9},{9,8},{10,11... | collective-permute-start | bytes 811016 | tf_op jit(solution)/shard_map/ppermute | solution.py:491
  24.4 8.9 %collective-permute-start.12 = (bf16[264,512]{1,0:T(8,128)(2,1)S(1)}, bf16[264,512]{1,0:T(8,128)(2,1)S(1)}, u32[]{:S(2)}, u32[]{:S(2)}) collective-permute-start(bf16[264,512]{1,0:T(8,128)(2,1)S(1)} %collective-permute-done.11.t0_ref), channel_id=1, source_target_pairs={{0,1},{1,0},{2,3},{3,2},{4,5},{5,4},{6,7},{7,6},{8,9},{9,8},{10,11... | collective-permute-start | bytes 811016 | tf_op jit(solution)/shard_map/ppermute | solution.py:491
  24.4 11.1 %collective-permute-start.6 = (bf16[272,512]{1,0:T(8,128)(2,1)S(1)}, bf16[272,512]{1,0:T(8,128)(2,1)S(1)}, u32[]{:S(2)}, u32[]{:S(2)}) collective-permute-start(bf16[272,512]{1,0:T(8,128)(2,1)S(1)} %get-tuple-element.36.refs_0_), channel_id=1, source_target_pairs={{0,4},{1,5},{2,6},{3,7},{4,0},{5,1},{6,2},{7,3},{8,12},{9,13},{10,... | collective-permute-start | bytes 835592 | tf_op jit(solution)/shard_map/ppermute | solution.py:491
  24.4 10.1 %collective-permute-start.8 = (bf16[256,512]{1,0:T(8,128)(2,1)}, bf16[256,512]{1,0:T(8,128)(2,1)S(1)}, u32[]{:S(2)}, u32[]{:S(2)}) collective-permute-start(bf16[256,512]{1,0:T(8,128)(2,1)} %refs_3_.1), channel_id=1, source_target_pairs={{0,16},{16,0},{1,17},{17,1},{2,18},{18,2},{3,19},{19,3},{4,20},{20... | collective-permute-start | bytes 786440 | tf_op jit(solution)/shard_map/ppermute | solution.py:495
  29.6 21.8 %collective-permute-start.3 = (bf16[272,512]{1,0:T(8,128)(2,1)S(1)}, bf16[272,512]{1,0:T(8,128)(2,1)S(1)}, u32[]{:S(2)}, u32[]{:S(2)}) collective-permute-start(bf16[272,512]{1,0:T(8,128)(2,1)S(1)} %collective-permute-done.1.refs_0_), channel_id=1, source_target_pairs={{0,4},{1,5},{2,6},{3,7},{4,0},{5,1},{6,2},{7,3},{8,12},{9,13},{10,... | collective-permute-start | bytes 835592 | tf_op jit(solution)/shard_map/ppermute | solution.py:491
  30.8 14.5 %collective-permute-start.13 = (bf16[128,512]{1,0:T(8,128)(2,1)S(1)}, bf16[128,512]{1,0:T(8,128)(2,1)S(1)}, u32[]{:S(2)}, u32[]{:S(2)}) collective-permute-start(bf16[128,512]{1,0:T(8,128)(2,1)S(1)} %get-tuple-element.44), channel_id=1, source_target_pairs={{0,6},{1,7},{2,4},{3,5},{4,2},{5,3},{6,0},{7,1},{8,14},{9,15},{10,... | collective-permute-start | bytes 393224 | tf_op jit(solution)/shard_map/ppermute | solution.py:491
  33.2 13.8 %collective-permute-start.14 = (bf16[128,512]{1,0:T(8,128)(2,1)S(1)}, bf16[128,512]{1,0:T(8,128)(2,1)S(1)}, u32[]{:S(2)}, u32[]{:S(2)}) collective-permute-start(bf16[128,512]{1,0:T(8,128)(2,1)S(1)} %get-tuple-element.45), channel_id=1, source_target_pairs={{0,4},{1,5},{2,6},{3,7},{4,0},{5,1},{6,2},{7,3},{8,12},{9,13},{10,... | collective-permute-start | bytes 393224 | tf_op jit(solution)/shard_map/ppermute | solution.py:491
  34.4 16.4 %collective-permute-start.15 = (bf16[128,512]{1,0:T(8,128)(2,1)S(1)}, bf16[128,512]{1,0:T(8,128)(2,1)S(1)}, u32[]{:S(2)}, u32[]{:S(2)}) collective-permute-start(bf16[128,512]{1,0:T(8,128)(2,1)S(1)} %get-tuple-element.46), channel_id=1, source_target_pairs={{0,2},{1,3},{2,0},{3,1},{4,6},{5,7},{6,4},{7,5},{8,10},{9,11},{10,... | collective-permute-start | bytes 393224 | tf_op jit(solution)/shard_map/ppermute | solution.py:491
  35.5 15.9 %collective-permute-start.20 = (bf16[128,512]{1,0:T(8,128)(2,1)S(1)}, bf16[128,512]{1,0:T(8,128)(2,1)S(1)}, u32[]{:S(2)}, u32[]{:S(2)}) collective-permute-start(bf16[128,512]{1,0:T(8,128)(2,1)S(1)} %get-tuple-element.52), channel_id=1, source_target_pairs={{0,6},{1,7},{2,4},{3,5},{4,2},{5,3},{6,0},{7,1},{8,14},{9,15},{10,... | collective-permute-start | bytes 393224 | tf_op jit(solution)/shard_map/ppermute | solution.py:491
  50.9 10.8 %collective-permute-start.5 = (bf16[272,512]{1,0:T(8,128)(2,1)S(1)}, bf16[272,512]{1,0:T(8,128)(2,1)S(1)}, u32[]{:S(2)}, u32[]{:S(2)}) collective-permute-start(bf16[272,512]{1,0:T(8,128)(2,1)S(1)} %get-tuple-element.36.refs_0_), channel_id=1, source_target_pairs={{0,2},{1,3},{2,0},{3,1},{4,6},{5,7},{6,4},{7,5},{8,10},{9,11},{10,... | collective-permute-start | bytes 835592 | tf_op jit(solution)/shard_map/ppermute | solution.py:491
  51.4 11.5 %collective-permute-start.9 = (bf16[256,512]{1,0:T(8,128)(2,1)S(1)}, bf16[256,512]{1,0:T(8,128)(2,1)S(1)}, u32[]{:S(2)}, u32[]{:S(2)}) collective-permute-start(bf16[256,512]{1,0:T(8,128)(2,1)S(1)} %collective-permute-done.8.refs_4_), channel_id=1, source_target_pairs={{0,1},{1,0},{2,3},{3,2},{4,5},{5,4},{6,7},{7,6},{8,9},{9,8},{10,11... | collective-permute-start | bytes 786440 | tf_op jit(solution)/shard_map/ppermute | solution.py:491
  51.4 26.0 %collective-permute-start.2 = (bf16[272,512]{1,0:T(8,128)(2,1)S(1)}, bf16[272,512]{1,0:T(8,128)(2,1)S(1)}, u32[]{:S(2)}, u32[]{:S(2)}) collective-permute-start(bf16[272,512]{1,0:T(8,128)(2,1)S(1)} %collective-permute-done.1.refs_0_), channel_id=1, source_target_pairs={{0,2},{1,3},{2,0},{3,1},{4,6},{5,7},{6,4},{7,5},{8,10},{9,11},{10,... | collective-permute-start | bytes 835592 | tf_op jit(solution)/shard_map/ppermute | solution.py:491
  53.0 19.4 %collective-permute-start.7 = (bf16[272,512]{1,0:T(8,128)(2,1)S(1)}, bf16[272,512]{1,0:T(8,128)(2,1)S(1)}, u32[]{:S(2)}, u32[]{:S(2)}) collective-permute-start(bf16[272,512]{1,0:T(8,128)(2,1)S(1)} %collective-permute-done.6.refs_2_), channel_id=1, source_target_pairs={{0,2},{1,3},{2,0},{3,1},{4,6},{5,7},{6,4},{7,5},{8,10},{9,11},{10,... | collective-permute-start | bytes 835592 | tf_op jit(solution)/shard_map/ppermute | solution.py:491
  54.2 24.2 %collective-permute-start.4 = (bf16[272,512]{1,0:T(8,128)(2,1)S(1)}, bf16[272,512]{1,0:T(8,128)(2,1)S(1)}, u32[]{:S(2)}, u32[]{:S(2)}) collective-permute-start(bf16[272,512]{1,0:T(8,128)(2,1)S(1)} %collective-permute-done.3.refs_2_), channel_id=1, source_target_pairs={{0,2},{1,3},{2,0},{3,1},{4,6},{5,7},{6,4},{7,5},{8,10},{9,11},{10,... | collective-permute-start | bytes 835592 | tf_op jit(solution)/shard_map/ppermute | solution.py:491
  61.7 18.7 %collective-permute-start.16 = (bf16[128,512]{1,0:T(8,128)(2,1)S(1)}, bf16[128,512]{1,0:T(8,128)(2,1)S(1)}, u32[]{:S(2)}, u32[]{:S(2)}) collective-permute-start(bf16[128,512]{1,0:T(8,128)(2,1)S(1)} %get-tuple-element.48), channel_id=1, source_target_pairs={{0,2},{1,3},{2,0},{3,1},{4,6},{5,7},{6,4},{7,5},{8,10},{9,11},{10,... | collective-permute-start | bytes 393224 | tf_op jit(solution)/shard_map/ppermute | solution.py:491
  62.9 18.5 %collective-permute-start.19 = (bf16[128,512]{1,0:T(8,128)(2,1)S(1)}, bf16[128,512]{1,0:T(8,128)(2,1)S(1)}, u32[]{:S(2)}, u32[]{:S(2)}) collective-permute-start(bf16[128,512]{1,0:T(8,128)(2,1)S(1)} %get-tuple-element.51), channel_id=1, source_target_pairs={{0,8},{1,9},{2,10},{3,11},{4,12},{5,13},{6,14},{7,15},{8,0},{9,1},... | collective-permute-start | bytes 393224 | tf_op jit(solution)/shard_map/ppermute | solution.py:491
  72.4 12.9 %collective-permute-start.24 = (bf16[128,512]{1,0:T(8,128)(2,1)S(1)}, bf16[128,512]{1,0:T(8,128)(2,1)S(1)}, u32[]{:S(2)}, u32[]{:S(2)}) collective-permute-start(bf16[128,512]{1,0:T(8,128)(2,1)S(1)} %get-tuple-element.56), channel_id=1, source_target_pairs={{0,12},{1,13},{2,14},{3,15},{4,8},{5,9},{6,10},{7,11},{8,4},{9,5},... | collective-permute-start | bytes 393224 | tf_op jit(solution)/shard_map/ppermute | solution.py:491
  79.3 17.9 %collective-permute-start.28 = (bf16[256,512]{1,0:T(8,128)(2,1)S(1)}, bf16[256,512]{1,0:T(8,128)(2,1)S(1)}, u32[]{:S(2)}, u32[]{:S(2)}) collective-permute-start(bf16[256,512]{1,0:T(8,128)(2,1)S(1)} %get-tuple-element.60), channel_id=1, source_target_pairs={{0,1},{1,0},{2,3},{3,2},{4,5},{5,4},{6,7},{7,6},{8,9},{9,8},{10,11... | collective-permute-start | bytes 786440 | tf_op jit(solution)/shard_map/ppermute | solution.py:491
  80.3 10.4 %collective-permute-start.18 = (bf16[128,512]{1,0:T(8,128)(2,1)S(1)}, bf16[128,512]{1,0:T(8,128)(2,1)S(1)}, u32[]{:S(2)}, u32[]{:S(2)}) collective-permute-start(bf16[128,512]{1,0:T(8,128)(2,1)S(1)} %get-tuple-element.50), channel_id=1, source_target_pairs={{0,6},{1,7},{2,4},{3,5},{4,2},{5,3},{6,0},{7,1},{8,14},{9,15},{10,... | collective-permute-start | bytes 393224 | tf_op jit(solution)/shard_map/ppermute | solution.py:491
  81.4 9.4 %collective-permute-start.23 = (bf16[128,512]{1,0:T(8,128)(2,1)S(1)}, bf16[128,512]{1,0:T(8,128)(2,1)S(1)}, u32[]{:S(2)}, u32[]{:S(2)}) collective-permute-start(bf16[128,512]{1,0:T(8,128)(2,1)S(1)} %get-tuple-element.55), channel_id=1, source_target_pairs={{0,10},{1,11},{2,8},{3,9},{4,14},{5,15},{6,12},{7,13},{8,2},{9,3},... | collective-permute-start | bytes 393224 | tf_op jit(solution)/shard_map/ppermute | solution.py:491
  85.3 10.3 %collective-permute-start.25 = (bf16[128,512]{1,0:T(8,128)(2,1)S(1)}, bf16[128,512]{1,0:T(8,128)(2,1)S(1)}, u32[]{:S(2)}, u32[]{:S(2)}) collective-permute-start(bf16[128,512]{1,0:T(8,128)(2,1)S(1)} %get-tuple-element.57), channel_id=1, source_target_pairs={{0,14},{1,15},{2,12},{3,13},{4,10},{5,11},{6,8},{7,9},{8,6},{9,7},... | collective-permute-start | bytes 393224 | tf_op jit(solution)/shard_map/ppermute | solution.py:491
  86.0 14.7 %collective-permute-start.26 = (bf16[256,512]{1,0:T(8,128)(2,1)S(1)}, bf16[256,512]{1,0:T(8,128)(2,1)S(1)}, u32[]{:S(2)}, u32[]{:S(2)}) collective-permute-start(bf16[256,512]{1,0:T(8,128)(2,1)S(1)} %shard_map.101), channel_id=1, source_target_pairs={{0,1},{1,0},{2,3},{3,2},{4,5},{5,4},{6,7},{7,6},{8,9},{9,8},{10,11... | collective-permute-start | bytes 786440 | tf_op jit(solution)/shard_map/ppermute | solution.py:491
  (7 other events, 40.8 us)
